TPU v7x, 256 devices: a whole 4x4x8 slice. The times are simulated.
256 devices in a mesh: gx: 8 (over x, core), gy: 32 (over z, y).
Axes of the slice: x: 4, y: 4, z: 8, core: 2. Of those that a mesh axis runs over, the one named last changes fastest.
Arguments:
- residual: float32 [1024, 1024, 256], P('gx', 'gy'), may hold values from -6 to 6
- local_x: bfloat16 [136, 136], replicated, may hold values from -0.5 to 0.5
- local_y: bfloat16 [40, 40], replicated, may hold values from -1 to 1
- local_z: bfloat16 [256, 256], replicated, may hold values from -0.375 to 0.375
- eig_x: float32 [136], replicated, may hold values from 0.1 to 2
- eig_y: float32 [40], replicated, may hold values from 0.1 to 2
- eig_z: float32 [256], replicated, may hold values from 0.1 to 2
- coarse_x: bfloat16 [128, 4], replicated, may hold values from -0.5 to 0.5
- coarse_y: bfloat16 [32, 4], replicated, may hold values from -1 to 1
- coarse_z: bfloat16 [256, 4], replicated, may hold values from -0.375 to 0.375
- mode_x: float32 [32, 32], replicated, may hold values from -1 to 1
- mode_y: float32 [128, 128], replicated, may hold values from -0.5 to 0.5
- mode_z: float32 [4, 4], replicated, may hold values from -3 to 3
- coarse_eig_x: float32 [32], replicated, may hold values from 0.002 to 0.02
- coarse_eig_y: float32 [128], replicated, may hold values from 0.002 to 0.02
- coarse_eig_z: float32 [4], replicated, may hold values from 0.002 to 0.02
Outputs:
- preconditioned: float32 [1024, 1024, 256], P('gx', 'gy')
All inputs are finite; a program needn't handle non-finite values.
Results may differ from a plain program's by a relative error of at most 0.0045.
Values may be sent and summed in bfloat16 or wider, within the bound.
No kernel may reach another device: no remote copies, remote signals or barrier semaphores. Data moves between devices by JAX's collectives and lax.ppermute only.
A program may use at most 64 MiB of HBM per device.

v0:
```python
import jax
import jax.numpy as jnp
from jax import lax
from jax.experimental import pallas as pl
from jax.experimental.pallas import tpu as pltpu
from jax.sharding import PartitionSpec as P


OV = 4
MODES = 4
CX = 128
CY = 32
NZ = 256
EX = 136
EY = 40
GX = 4
ROWS = GX * EY
OWN = GX * CY
RIM = GX * OV
BLOCKS = CX // GX
CELLS = CX * CY
CHUNKS = 8
WIDE_LOAD = 50
WIDE_SOLVE = 48
HI = lax.Precision.HIGHEST
f32 = jnp.float32
bf16 = jnp.bfloat16
sds = jax.ShapeDtypeStruct

VM = pl.BlockSpec(memory_space=pltpu.VMEM)
SM = pl.BlockSpec(memory_space=pltpu.SMEM)
ANY = pl.BlockSpec(memory_space=pl.ANY)
HBM = pl.BlockSpec(memory_space=pltpu.HBM)


def dot(a, b):
    return jnp.dot(a, b, preferred_element_type=f32)


def dot_t(a, b):
    return lax.dot_general(a, b, (((1,), (1,)), ((), ())), preferred_element_type=f32)


def dot_hi(a, b):
    return jnp.dot(a, b, preferred_element_type=f32, precision=HI)


def dot_t_hi(a, b):
    dims = (((1,), (1,)), ((), ()))
    return lax.dot_general(a, b, dims, preferred_element_type=f32, precision=HI)


def split(x):
    high = x.astype(bf16)
    return high, (x - high.astype(f32)).astype(bf16)


def split3(x):
    high = x.astype(bf16)
    rest = x - high.astype(f32)
    middle = rest.astype(bf16)
    return high, middle, (rest - middle.astype(f32)).astype(bf16)


def expand(x, rows=None, cols=None):
    parts = split3(x)
    if rows is not None:
        return dot(jnp.concatenate([rows] * 3, 1), jnp.concatenate(parts, 0))
    return dot(jnp.concatenate(parts, 1), jnp.concatenate([cols] * 3, 0))


def iotas(shape):
    return lax.broadcasted_iota(jnp.int32, shape, 0), lax.broadcasted_iota(jnp.int32, shape, 1)


def pick(mask, kind=bf16):
    return jnp.where(mask, 1.0, 0.0).astype(kind)


def call(kernel, out_shape, in_specs, mib, out_specs=None, scratch=()):
    if out_specs is None:
        out_specs = jax.tree.map(lambda _: VM, out_shape)
    return pl.pallas_call(
        kernel,
        out_shape=out_shape,
        in_specs=in_specs,
        out_specs=out_specs,
        scratch_shapes=list(scratch),
        compiler_params=pltpu.CompilerParams(vmem_limit_bytes=mib << 20),
    )


def tile(ref, k, rows):
    return ref[pl.ds(pl.multiple_of(k * rows, rows), rows), :]


def selection(cyt):
    row, col = iotas((3 * RIM, OWN))
    y, k = iotas((CY, OWN))
    spread = dot(cyt, pick((k & 31) == y)).astype(bf16)
    row4, n = iotas((3 * RIM, MODES))
    modes = dot(pick((row4 & 3) == n), spread)
    plane = ((row >> 2) & 3) == (col >> 5)
    inner = col & 31
    target = jnp.where(row < RIM, row & 3, CY - OV + (row & 3))
    ones = jnp.where(inner == target, 1.0, 0.0)
    value = jnp.where(row < 2 * RIM, ones, modes)
    return jnp.where(plane, value, 0.0).astype(bf16)


def load_kernel(
    residual, cyt, first_x, last_x, rim_lo, rim_hi, along_y, sel, buf, sems, cyt_buf, sem
):
    rows = CELLS // CHUNKS

    def copy(c):
        at = pl.ds(c * rows, rows)
        return pltpu.make_async_copy(residual.at[at, :], buf.at[at, :], sems.at[c])

    for c in range(CHUNKS):
        copy(c).start()
    small = pltpu.make_async_copy(cyt, cyt_buf, sem)
    small.start()
    small.wait()
    take = selection(cyt_buf[...])
    sel[...] = take
    for c in range(CHUNKS):
        copy(c).wait()
        for b in range(rows // OWN):
            k = c * (rows // OWN) + b
            data = buf[k * OWN : (k + 1) * OWN, :].astype(bf16)
            if k == 0:
                first_x[...] = data
            if k == BLOCKS - 1:
                last_x[...] = data
            out = dot(take, data)
            at = slice(k * RIM, (k + 1) * RIM)
            rim_lo[at, :] = out[:RIM].astype(bf16)
            rim_hi[at, :] = out[RIM : 2 * RIM].astype(bf16)
            along_y[at, :] = out[2 * RIM :]


def load(residual, coarse_y):
    rim = sds((CX * OV, NZ), bf16)
    return call(
        load_kernel,
        (
            sds((OWN, NZ), bf16), sds((OWN, NZ), bf16), rim, rim,
            sds((CX * MODES, NZ), f32), sds((3 * RIM, OWN), bf16),
        ),
        [HBM, HBM],
        WIDE_LOAD,
        scratch=[
            pltpu.VMEM((CELLS, NZ), f32), pltpu.SemaphoreType.DMA((CHUNKS,)),
            pltpu.VMEM((MODES, CY), bf16), pltpu.SemaphoreType.DMA,
        ],
    )(residual, coarse_y.T)


def corners_kernel(sel, rim_lo, rim_hi, xlo, xhi, after, down, up):
    down[: CX * OV, :] = rim_lo[...]
    up[: CX * OV, :] = rim_hi[...]
    for i, strip in enumerate((xlo, xhi)):
        out = dot(sel[: 2 * RIM, :], strip[...]).astype(bf16)
        at = slice(CX * OV + i * RIM, CX * OV + (i + 1) * RIM)
        down[at, :] = out[:RIM]
        up[at, :] = out[RIM:]


def corners(*args):
    side = sds((EX * OV, NZ), bf16)
    return call(corners_kernel, (side, side), [VM] * 5 + [ANY], 8)(*args)


PARAMS = (
    ((EX, EX), bf16), ((EY, EY), bf16), ((NZ, NZ), bf16), ((1, EX), f32), ((1, EY), f32),
    ((1, NZ), f32), ((MODES, CY), bf16),
)
WEIGHTS = (
    ((ROWS, ROWS), bf16), ((ROWS, ROWS), bf16), ((OWN, ROWS + 2 * RIM), bf16),
    ((OWN // 2, 2 * RIM), bf16), ((EX, EX), bf16),
    ((EX, EX), bf16), ((NZ, NZ), bf16), ((NZ, NZ), bf16), ((EX, NZ), f32), ((EY, NZ), f32),
)


def basis_x(cxt):
    x, row = iotas((CX, CX * MODES))
    by_row = dot(cxt, pick((row >> 2) == x)).astype(bf16)
    col, m = iotas((16, MODES))
    value = dot(pick((col >> 2) == m), by_row)
    col, row = iotas((16, CX * MODES))
    return jnp.where((row & 3) == (col & 3), value, 0.0).astype(bf16)


def spread_z(mode_z):
    row, col = iotas((128, 128))
    out = jnp.zeros((128, 128), f32)
    for p in range(MODES):
        for c in range(MODES):
            here = ((row & 3) == p) & ((col & 3) == c)
            out = jnp.where(here, mode_z[p : p + 1, c : c + 1], out)
    return out


def modes_a():
    a, col = iotas((32, 128))
    c, col4 = iotas((MODES, 128))
    return pick((col >> 2) == a), pick((col4 & 3) == c)


def prepare_kernel(*refs):
    n = len(PARAMS)
    sources, outs, bufs, sems = (
        refs[:n], refs[n + 1 : n + 1 + len(WEIGHTS)], refs[n + 1 + len(WEIGHTS) : -1], refs[-1]
    )
    copies = [
        pltpu.make_async_copy(source, buf, sems.at[i])
        for i, (source, buf) in enumerate(zip(sources, bufs))
    ]
    for copy in copies:
        copy.start()
    for copy in copies:
        copy.wait()
    lx, ly, lz, eig_x, eig_y, eig_z, cyt = bufs
    wy, wyt, wfin, spread, wx, wxt, lz_out, lzt, exb, eyz = outs

    def cell(k):
        y = jnp.where(k < OWN, OV + (k & 31), jnp.where(k < OWN + RIM, k & 3, EY - OV + (k & 3)))
        plane = jnp.where(k < OWN, k >> 5, ((k - OWN) >> 2) & 3)
        return y, plane

    def mode(j):
        plane = (j >= EY).astype(jnp.int32) + (j >= 2 * EY) + (j >= 3 * EY)
        return j - EY * plane, plane

    k, y = iotas((ROWS, EY))
    by_cell = dot(pick(cell(k)[0] == y), ly[...]).astype(bf16)
    b, j = iotas((EY, ROWS))
    k, col = iotas((ROWS, ROWS))
    value = dot(by_cell, pick(mode(j)[0] == b))
    value = jnp.where(cell(k)[1] == mode(col)[1], value, 0.0).astype(bf16)
    wyt[...] = value
    j, b = iotas((ROWS, EY))
    back = dot_t(pick(mode(j)[0] == b), by_cell)
    wy[...] = jnp.where(mode(k)[1] == cell(col)[1], back, 0.0).astype(bf16)

    y, k = iotas((CY, OWN))
    by_k = dot(cyt[...], pick((k & 31) == y)).astype(bf16)
    k, own = iotas((OWN, OWN))
    turned = dot_t(pick(k == own), by_k).astype(bf16)
    n, col = iotas((MODES, 2 * RIM))
    coarse = dot(turned, pick((col & 3) == n))
    k, col = iotas((OWN, 2 * RIM))
    inner = k & 31
    plane = (k >> 5) == ((col >> 2) & 3)
    coarse = jnp.where(plane, coarse, 0.0).astype(bf16)
    wfin[...] = jnp.concatenate([value[:OWN], coarse], 1)
    k, col = iotas((OWN // 2, 2 * RIM))
    inner = (k & 15) + jnp.where((k & 15) < 8, 0, CY - 16)
    target = jnp.where(col < RIM, col & 3, CY - OV + (col & 3))
    ones = jnp.where(inner == target, 1.0, 0.0)
    spread[...] = jnp.where((k >> 4) == ((col >> 2) & 3), ones, 0.0).astype(bf16)

    k, x = iotas((EX, EX))
    source = jnp.where(k < CX, k + OV, jnp.where(k < CX + OV, k - CX, k))
    moved = dot(pick(source == x), lx[...]).astype(bf16)
    wxt[...] = moved
    wx[...] = dot_t(pick(k == x), moved).astype(bf16)
    column = jnp.sum(jnp.where(k == x, eig_x[...], 0.0), axis=1, keepdims=True)
    exb[...] = jnp.broadcast_to(column, (EX, NZ))
    b, y = iotas((EY, EY))
    column = jnp.sum(jnp.where(b == y, eig_y[...], 0.0), axis=1, keepdims=True)
    eyz[...] = column + eig_z[...]
    c, z = iotas((NZ, NZ))
    lz_out[...] = lz[...]
    lzt[...] = dot_t(pick(c == z), lz[...]).astype(bf16)


def prepare(*params):
    return call(
        prepare_kernel,
        tuple(sds(*w) for w in WEIGHTS),
        [HBM] * len(PARAMS) + [ANY],
        8,
        scratch=[pltpu.VMEM(*p) for p in PARAMS] + [pltpu.SemaphoreType.DMA((len(PARAMS),))],
    )(*params)


def solve_kernel(
    residual, xlo, xhi, ylo, yhi, wy, wyt, wx, wxt, lz, lzt, exb, eyz, after,
    kept, out_xlo, out_xhi, out_ylo, out_yhi, field, mid, spec, buf, sems,
):
    def put(rows, value):
        field[0, rows, :] = value[:, :128]
        field[1, rows, :] = value[:, 128:]

    def take(rows):
        return jnp.concatenate([field[0, rows, :], field[1, rows, :]], 1)

    def forward_y(main, k):
        data = jnp.concatenate([main, tile(ylo, k, RIM), tile(yhi, k, RIM)], 0)
        put(pl.ds(pl.multiple_of(k * ROWS, ROWS), ROWS), dot(wy[...], data))

    rows = CELLS // CHUNKS
    per = BLOCKS // CHUNKS

    def copy(c):
        at = pl.ds(pl.multiple_of(c * rows, rows), rows)
        return pltpu.make_async_copy(residual.at[at, :], buf.at[at, :], sems.at[c])

    for c in range(CHUNKS):
        copy(c).start()

    def first(c, carry):
        for i in range(2):
            copy(2 * c + i).wait()
        for b in range(2 * per):
            k = c * 2 * per + b
            forward_y(tile(buf, k, OWN).astype(bf16), k)
        return carry

    lax.fori_loop(0, CHUNKS // 2, first, 0)
    forward_y(xlo[...], BLOCKS)
    forward_y(xhi[...], BLOCKS + 1)

    def mid_rows(b):
        return pl.ds(pl.multiple_of(b * EX, 8), EX)

    def forward_x(b, carry):
        plane = take(pl.ds(b, EX, stride=EY)).astype(bf16)
        mid[mid_rows(b), :] = dot(wx[...], plane)
        return carry

    lax.fori_loop(0, EY, forward_x, 0, unroll=40)

    def forward_z(i, carry):
        at = pl.ds(pl.multiple_of(i * 4 * EX, 16), 4 * EX)
        along = dot(mid[at, :].astype(bf16), lz[...])
        parts = []
        for q in range(4):
            scale = exb[...] + eyz[pl.ds(i * 4 + q, 1), :]
            parts.append((along[q * EX : (q + 1) * EX] / scale))
        spec[at, :] = jnp.concatenate(parts, 0).astype(bf16)
        return carry

    lax.fori_loop(0, EY // 4, forward_z, 0, unroll=10)

    def backward_z(i, carry):
        at = pl.ds(pl.multiple_of(i * 4 * EX, 16), 4 * EX)
        mid[at, :] = dot(spec[at, :], lzt[...])
        return carry

    lax.fori_loop(0, EY // 4, backward_z, 0, unroll=10)

    def backward_x(b, carry):
        put(pl.ds(b, EX, stride=EY), dot(wxt[...], mid[mid_rows(b), :].astype(bf16)))
        return carry

    lax.fori_loop(0, EY, backward_x, 0, unroll=40)

    def planes(k):
        return take(pl.ds(pl.multiple_of(k * ROWS, ROWS), ROWS)).astype(bf16)

    out_xlo[...] = dot(wyt[...], planes(BLOCKS)).astype(bf16)
    out_xhi[...] = dot(wyt[...], planes(BLOCKS + 1)).astype(bf16)

    def last(k, carry):
        data = planes(k)
        kept[pl.ds(pl.multiple_of(k * ROWS, ROWS), ROWS), :] = data
        out = dot(wyt[OWN:, :], data).astype(bf16)
        at = pl.ds(pl.multiple_of(k * RIM, RIM), RIM)
        out_ylo[at, :] = out[:RIM]
        out_yhi[at, :] = out[RIM:]
        return carry

    lax.fori_loop(0, BLOCKS, last, 0, unroll=16)


def solve(*args):
    strip = sds((ROWS, NZ), bf16)
    rim = sds((CX * OV, NZ), bf16)
    return call(
        solve_kernel,
        (sds((BLOCKS * ROWS, NZ), bf16), strip, strip, rim, rim),
        [HBM] + [VM] * 12 + [ANY],
        WIDE_SOLVE,
        scratch=[
            pltpu.VMEM((2, EX * EY, NZ // 2), f32), pltpu.VMEM((EX * EY, NZ), f32),
            pltpu.VMEM((EX * EY, NZ), bf16), pltpu.VMEM((CELLS, NZ), f32),
            pltpu.SemaphoreType.DMA((CHUNKS,)),
        ],
    )(*args)


def fold_kernel(out_ylo, out_yhi, rxlo, rxhi, down, up):
    end = CX * OV
    for strip, start, out in ((out_ylo, OWN, down), (out_yhi, OWN + RIM, up)):
        rows = slice(start, start + RIM)
        out[...] = strip[...]
        low = strip[:RIM, :].astype(f32) + rxlo[rows, :].astype(f32)
        high = strip[end - RIM :, :].astype(f32) + rxhi[rows, :].astype(f32)
        out[:RIM, :] = low.astype(bf16)
        out[end - RIM :, :] = high.astype(bf16)


def fold(*args):
    rim = sds((CX * OV, NZ), bf16)
    return call(fold_kernel, (rim, rim), [VM] * 4, 8)(*args)


def restrict_kernel(along_y, cxt, czt, mode_x, mode_z, out, modes_xz):
    bx = basis_x(cxt[...])
    high, low = split(along_y[...])
    both = dot(bx, high) + dot(bx, low)
    own = dot_t_hi(both, czt[...].astype(f32))
    flat = jnp.concatenate([own[m * MODES : (m + 1) * MODES] for m in range(MODES)], 1)
    for i in range(out.shape[0]):
        out[i] = flat
    to_a, _ = modes_a()
    r, i = iotas((128, 32))
    part_x = expand(expand(mode_x[...], rows=pick((r >> 2) == i)), cols=to_a)
    part_z = spread_z(mode_z[...])
    modes_xz[...] = part_x * part_z


def coarse_x_kernel(rows, modes_xz, out):
    part = dot_hi(jnp.concatenate([rows[i] for i in range(8)], 1), modes_xz[...])
    for i in range(out.shape[0]):
        out[i] = part


def coarse_kernel(rows, modes_xz, mode_y, ceig_x, ceig_y, ceig_z, cxt, czt, after, out):
    to_a, to_c = modes_a()
    eight_x = jnp.broadcast_to(ceig_x[...], (8, 32))
    eight_z = jnp.broadcast_to(ceig_z[...], (8, MODES))
    row = (dot_hi(eight_x, to_a.astype(f32)) + dot_hi(eight_z, to_c.astype(f32)))[:1]
    r, b = iotas((128, 128))
    column = jnp.sum(jnp.where(r == b, ceig_y[...], 0.0), axis=1, keepdims=True)
    columns = jnp.concatenate([rows[j] for j in range(rows.shape[0])], 0)
    hat = dot_hi(mode_y[...].T, columns) / (column + row)
    row, col = iotas((8, 128))
    mine = pick(col == lax.axis_index("gy") * MODES + row, f32)
    rows_y = dot_hi(mine, mode_y[...])
    rows_xz = modes_xz[pl.ds(pl.multiple_of(lax.axis_index("gx") * 16, 16), 16), :]
    sol = dot_t_hi(dot_hi(rows_y, hat), rows_xz)
    levels = czt[...].astype(f32)
    shape = jnp.concatenate(
        [dot_hi(sol[:, m * MODES : (m + 1) * MODES], levels)[:MODES] for m in range(MODES)], 0
    )
    high, low = split(shape)
    col, i = iotas((32, 16))
    twice = dot(pick((col & 15) == i), basis_x(cxt[...]))
    value = dot(twice.T.astype(bf16), jnp.concatenate([high, low], 0))
    high, low = split(value)
    for k in range(BLOCKS):
        at = slice(k * RIM, (k + 1) * RIM)
        out[2 * k * RIM : (2 * k + 1) * RIM, :] = high[at]
        out[(2 * k + 1) * RIM : (2 * k + 2) * RIM, :] = low[at]


def inner_copy(buf, out, sems, c):
    at = pl.ds(pl.multiple_of(c * (CX // CHUNKS), CX // CHUNKS), CX // CHUNKS)
    inner = pl.ds(8, CY - 16)
    return pltpu.make_async_copy(buf.at[at, inner, :], out.at[at, inner, :], sems.at[c])


def finish_kernel(field, wfin, shape, rxlo, rxhi, after, out, rims, buf, sems):
    per = BLOCKS // CHUNKS

    def block(k, extra):
        data = jnp.concatenate([tile(field, k, ROWS), tile(shape, k, 2 * RIM)], 0)
        total = dot(wfin[...], data)
        if extra is not None:
            total = total + extra[:OWN, :].astype(f32)
        total = total.reshape(GX, CY, NZ)
        planes = pl.ds(pl.multiple_of(k * GX, GX), GX)
        buf[planes, :, :] = total
        rims[planes, :8, :] = total[:, :8]
        rims[planes, 8:, :] = total[:, CY - 8 :]

    def step(c, carry):
        for b in range(per):
            block(c * per + b, None)
        inner_copy(buf, out, sems, c).start()
        return carry

    for b in range(per):
        block(b, rxlo if b == 0 else None)
    inner_copy(buf, out, sems, 0).start()
    lax.fori_loop(1, CHUNKS - 1, step, 0, unroll=2)
    for b in range(per):
        block(BLOCKS - per + b, rxhi if b == per - 1 else None)
    inner_copy(buf, out, sems, CHUNKS - 1).start()
    for c in range(CHUNKS):
        inner_copy(buf, out, sems, c).wait()


def finish(*args):
    return call(
        finish_kernel,
        (sds((CX, CY, NZ), f32), sds((CX, 16, NZ), f32)),
        [VM] * 5 + [ANY],
        16,
        out_specs=(HBM, VM),
        scratch=[pltpu.VMEM((CX, CY, NZ), f32), pltpu.SemaphoreType.DMA((CHUNKS,))],
    )(*args)


def combine_kernel(partial, rims, spread, rylo, ryhi, out, buf, sems):
    planes = CX // CHUNKS
    per = BLOCKS // CHUNKS

    def copies(c):
        at = pl.ds(c * planes, planes)
        return [
            pltpu.make_async_copy(
                buf.at[at, pl.ds(8 * i, 8), :], out.at[at, pl.ds(i * (CY - 8), 8), :],
                sems.at[2 * c + i],
            )
            for i in range(2)
        ]

    for c in range(CHUNKS):
        for b in range(per):
            k = c * per + b
            rim = slice(k * RIM, (k + 1) * RIM)
            data = jnp.concatenate([rylo[rim, :], ryhi[rim, :]], 0)
            strips = dot(spread[...], data).reshape(GX, 16, NZ)
            at = slice(k * GX, (k + 1) * GX)
            buf[at] = rims[at] + strips
        for copy in copies(c):
            copy.start()
    for c in range(CHUNKS):
        for copy in copies(c):
            copy.wait()


def combine(*args):
    return pl.pallas_call(
        combine_kernel,
        out_shape=sds((CX, CY, NZ), f32),
        in_specs=[HBM] + [VM] * 4,
        out_specs=HBM,
        scratch_shapes=[pltpu.VMEM((CX, 16, NZ), f32), pltpu.SemaphoreType.DMA((2 * CHUNKS,))],
        input_output_aliases={0: 0},
        compiler_params=pltpu.CompilerParams(vmem_limit_bytes=16 << 20),
        name="combine",
    )(*args)


def shift(x, axis, step):
    size = lax.axis_size(axis)
    return lax.ppermute(x, axis, [(i, (i + step) % size) for i in range(size)])


def exchange(x, axis):
    return lax.all_to_all(x, axis, 0, 0)


def local(
    residual, local_x, local_y, local_z, eig_x, eig_y, eig_z, coarse_x, coarse_y, coarse_z,
    mode_x, mode_y, mode_z, coarse_eig_x, coarse_eig_y, coarse_eig_z,
):
    cells = residual.reshape(CELLS, NZ)
    first_x, last_x, rim_lo, rim_hi, along_y, sel = load(cells, coarse_y)
    xlo = shift(last_x, "gx", 1)
    xhi = shift(first_x, "gx", -1)
    own_coarse, modes_xz = call(
        restrict_kernel, (sds((8, MODES, 16), f32), sds((128, 128), f32)), [VM] * 5, 8
    )(along_y, coarse_x.T, coarse_z.T, mode_x, mode_z)
    rows = exchange(own_coarse, "gx")
    down, up = corners(sel, rim_lo, rim_hi, xlo, xhi, own_coarse)
    ylo = shift(up, "gy", 1)
    yhi = shift(down, "gy", -1)
    part = call(coarse_x_kernel, sds((32, MODES, 128), f32), [VM] * 2, 4)(rows, modes_xz)
    rows = exchange(part, "gy")

    wy, wyt, wfin, spread, wx, wxt, lz, lzt, exb, eyz = prepare(
        local_x, local_y, local_z, eig_x[None], eig_y[None], eig_z[None], coarse_y.T, part
    )
    field, out_xlo, out_xhi, out_ylo, out_yhi = solve(
        cells, xlo, xhi, ylo, yhi, wy, wyt, wx, wxt, lz, lzt, exb, eyz, part
    )

    rxlo = shift(out_xhi, "gx", 1)
    rxhi = shift(out_xlo, "gx", -1)
    down, up = fold(out_ylo, out_yhi, rxlo, rxhi)
    rylo = shift(up, "gy", 1)
    ryhi = shift(down, "gy", -1)
    shape = call(coarse_kernel, sds((2 * CX * MODES, NZ), bf16), [VM] * 8 + [ANY], 8)(
        rows, modes_xz, mode_y, coarse_eig_x[None], coarse_eig_y[None], coarse_eig_z[None],
        coarse_x.T, coarse_z.T, up,
    )
    partial, rims = finish(field, wfin, shape, rxlo, rxhi, up)
    return combine(partial, rims, spread, rylo, ryhi)


def solution(mesh):
    cells = P("gx", "gy", None)

    return jax.shard_map(
        local, mesh=mesh, in_specs=(cells,) + (P(),) * 15, out_specs=cells, check_vma=False
    )
```

profile of v0, /device:TPU:1, one launch (start us, length us, event | category | flops | bytes accessed | tf_op | source)
XLA Modules:
  0.0 64.3 jit_solution(4320539498086538147)
XLA Ops:
  0.0 0.0 copy-start.4
  0.0 0.0 copy-start.1
  0.0 0.0 copy-start.6
  0.0 0.7 %copy-done.6 = bf16[32,4]{0,1:T(4,128)(2,1)S(1)} copy-done((bf16[32,4]{0,1:T(4,128)(2,1)S(1)}, bf16[32,4]{0,1:T(4,128)(2,1)}, u32[]{:S(2)}) %copy-start.6) | copy-done | bytes 280
  0.8 0.0 copy-start.14
  0.8 2.5 %shard_map.154 = (bf16[128,256]{1,0:T(8,128)(2,1)S(1)}, bf16[128,256]{1,0:T(8,128)(2,1)S(1)}, bf16[512,256]{1,0:T(8,128)(2,1)S(1)}, bf16[512,256]{1,0:T(8,128)(2...) custom-call(f32[4096,256]{1,0:T(8,128)} %bitcast.22, bf16[4,32]{1,0:T(4,128)(2,1)S(1)} %bitcast.12), custom_call_target="tpu_custom_call" | custom-call | tf_op jit(solution)/shard_map/pallas_call | solution.py:145
  3.3 0.0 copy-start.2
  3.4 0.0 copy-start.11
  3.4 0.0 copy-start.12
  3.4 0.0 copy-start.13
  3.4 2.6 %collective-permute-start = (bf16[128,256]{1,0:T(8,128)(2,1)S(1)}, bf16[128,256]{1,0:T(8,128)(2,1)S(1)}, u32[]{:S(2)}, u32[]{:S(2)}) collective-permute-start(bf16[128,256]{1,0:T(8,128)(2,1)S(1)} %get-tuple-element.34), channel_id=1, source_target_pairs={{0,32},{32,64},{64,96},{96,128},{128,160},{160,192},{192,224},{224... | collective-permute-start | bytes 196616 | tf_op jit(solution)/shard_map/ppermute | solution.py:553
  6.0 0.6 collective-permute-start.1
  6.6 0.0 copy-done.3
  6.6 0.0 copy-done.5
  6.6 0.0 copy-done.7
  6.6 0.0 copy-done.8
  6.6 0.8 %shard_map.155 = (f32[8,4,16]{2,1,0:T(4,128)S(1)}, f32[128,128]{1,0:T(8,128)S(1)}) custom-call(f32[512,256]{1,0:T(8,128)S(1)} %get-tuple-element.39.along_y, bf16[4,128]{1,0:T(4,128)(2,1)S(1)} %bitcast.14, bf16[4,256]{1,0:T(4,128)(2,1)S(1)} %bitcast.10, f32[32,32]{1,0:T(8,128)S(1)} %copy-done.3, f32[4,4]{1,0:T(4,128)S(1)} %copy-done.8), custom_call_target="tpu_custom_call" | custom-call | tf_op jit(solution)/shard_map/pallas_call | solution.py:568
  7.4 0.0 collective-permute-done.xlo
  7.4 2.2 %collective-permute-done.1.xhi = bf16[128,256]{1,0:T(8,128)(2,1)S(1)} collective-permute-done((bf16[128,256]{1,0:T(8,128)(2,1)S(1)}, bf16[128,256]{1,0:T(8,128)(2,1)S(1)}, u32[]{:S(2)}, u32[]{:S(2)}) %collective-permute-start.1) | collective-permute-done | bytes 65568 | tf_op jit(solution)/shard_map/ppermute | solution.py:553
  9.7 0.1 shard_map.156
  9.8 1.3 %collective-permute-start.2 = (bf16[544,256]{1,0:T(8,128)(2,1)S(1)}, bf16[544,256]{1,0:T(8,128)(2,1)S(1)}, u32[]{:S(2)}, u32[]{:S(2)}) collective-permute-start(bf16[544,256]{1,0:T(8,128)(2,1)S(1)} %get-tuple-element.41), channel_id=1, source_target_pairs={{0,1},{1,2},{2,3},{3,4},{4,5},{5,6},{6,7},{7,8},{8,9},{9,10},{10,1... | collective-permute-start | bytes 835592 | tf_op jit(solution)/shard_map/ppermute | solution.py:553
  11.2 6.8 %collective-permute-start.3 = (bf16[544,256]{1,0:T(8,128)(2,1)S(1)}, bf16[544,256]{1,0:T(8,128)(2,1)S(1)}, u32[]{:S(2)}, u32[]{:S(2)}) collective-permute-start(bf16[544,256]{1,0:T(8,128)(2,1)S(1)} %get-tuple-element.42), channel_id=1, source_target_pairs={{0,31},{1,0},{2,1},{3,2},{4,3},{5,4},{6,5},{7,6},{8,7},{9,8},{10,9... | collective-permute-start | bytes 835592 | tf_op jit(solution)/shard_map/ppermute | solution.py:553
  18.0 8.8 %all_to_all.10.rows = f32[8,4,16]{2,1,0:T(4,128)S(1)} all-to-all(f32[8,4,16]{2,1,0:T(4,128)S(1)} %get-tuple-element.40.after), channel_id=1, replica_groups=mesh['gx'=8,'gy'=32] {'gx'}, dimensions={0} | all-to-all | bytes 4096 | tf_op jit(solution)/shard_map/all_to_all | solution.py:557
  26.8 0.2 shard_map.157.refs_7_.after
  27.0 0.0 copy-done
  27.0 0.0 copy-done.4
  27.0 0.0 copy-done.1
  27.0 0.0 copy-done.9
  27.0 0.0 copy-done.10
  27.0 0.0 copy-done.14
  27.1 1.0 %shard_map.158 = (bf16[160,160]{1,0:T(8,128)(2,1)S(1)}, bf16[160,160]{1,0:T(8,128)(2,1)S(1)}, bf16[128,192]{1,0:T(8,128)(2,1)S(1)}, bf16[64,32]{1,0:T(8,128)(2,1...) custom-call(bf16[136,136]{1,0:T(8,128)(2,1)S(1)} %copy-done.1, ...), custom_call_target="tpu_custom_call" | custom-call | tf_op jit(solution)/shard_map/pallas_call | solution.py:280
  28.0 0.0 collective-permute-done.2.ylo
  28.0 0.0 collective-permute-done.3.yhi
  28.0 7.7 %shard_map.159 = (bf16[5120,256]{1,0:T(8,128)(2,1)S(1)}, bf16[160,256]{1,0:T(8,128)(2,1)S(1)}, bf16[160,256]{1,0:T(8,128)(2,1)S(1)}, bf16[512,256]{1,0:T(8,128)(2,1)S(1)}, bf16[512,256]{1,0:T(8,128)(2,1)S(1)}) custom-call(f32[4096,256]{1,0:T(8,128)} %bitcast.23, bf16[128,256]{1,0:T(8,128)(2,1)S(1)} %collective-permute-done.xlo, ...), custom_call_target="tpu_custom_call" | custom-call | tf_op jit(solution)/shard_map/pallas_call | solution.py:382
  35.8 0.9 %collective-permute-start.4 = (bf16[160,256]{1,0:T(8,128)(2,1)S(1)}, bf16[160,256]{1,0:T(8,128)(2,1)S(1)}, u32[]{:S(2)}, u32[]{:S(2)}) collective-permute-start(bf16[160,256]{1,0:T(8,128)(2,1)S(1)} %get-tuple-element.56), channel_id=1, source_target_pairs={{0,32},{32,64},{64,96},{96,128},{128,160},{160,192},{192,224},{224... | collective-permute-start | bytes 245768 | tf_op jit(solution)/shard_map/ppermute | solution.py:553
  36.7 0.0 collective-permute-start.5
  36.7 1.5 %collective-permute-done.4.rxlo = bf16[160,256]{1,0:T(8,128)(2,1)S(1)} collective-permute-done((bf16[160,256]{1,0:T(8,128)(2,1)S(1)}, bf16[160,256]{1,0:T(8,128)(2,1)S(1)}, u32[]{:S(2)}, u32[]{:S(2)}) %collective-permute-start.4) | collective-permute-done | bytes 81952 | tf_op jit(solution)/shard_map/ppermute | solution.py:553
  38.2 2.7 %collective-permute-done.5.rxhi = bf16[160,256]{1,0:T(8,128)(2,1)S(1)} collective-permute-done((bf16[160,256]{1,0:T(8,128)(2,1)S(1)}, bf16[160,256]{1,0:T(8,128)(2,1)S(1)}, u32[]{:S(2)}, u32[]{:S(2)}) %collective-permute-start.5) | collective-permute-done | bytes 81952 | tf_op jit(solution)/shard_map/ppermute | solution.py:553
  40.9 1.5 %collective-permute-start.7 = (bf16[512,256]{1,0:T(8,128)(2,1)S(1)}, bf16[512,256]{1,0:T(8,128)(2,1)S(1)}, u32[]{:S(2)}, u32[]{:S(2)}) collective-permute-start(bf16[512,256]{1,0:T(8,128)(2,1)S(1)} %get-tuple-element.62), channel_id=1, source_target_pairs={{0,31},{1,0},{2,1},{3,2},{4,3},{5,4},{6,5},{7,6},{8,7},{9,8},{10,9... | collective-permute-start | bytes 786440 | tf_op jit(solution)/shard_map/ppermute | solution.py:553
  42.3 0.1 collective-permute-start.6
  42.4 16.6 %all_to_all.11.rows = f32[32,4,128]{2,1,0:T(4,128)S(1)} all-to-all(f32[32,4,128]{2,1,0:T(4,128)S(1)} %shard_map.157.refs_7_.after), channel_id=1, replica_groups=mesh['gx'=8,'gy'=32] {'gy'}, dimensions={0} | all-to-all | bytes 131072 | tf_op jit(solution)/shard_map/all_to_all | solution.py:557
  59.0 0.0 copy-done.2
  59.1 0.0 copy-done.13
  59.1 1.5 %shard_map.161.shape = bf16[1024,256]{1,0:T(8,128)(2,1)S(1)} custom-call(f32[32,4,128]{2,1,0:T(4,128)S(1)} %all_to_all.11.rows, f32[128,128]{1,0:T(8,128)S(1)} %get-tuple-element.43.modes_xz, f32[128,128]{1,0:T(8,128)S(1)} %copy-done.2, f32[1,32]{1,0:T(1,128)S(1)} %bitcast.18, f32[1,128]{1,0:T(1,128)S(1)} %bitcast.19, f32[1,4]{1,0:T(1,128)S(1)} %bitcast.20, ...), custom_call_target="tpu_custom_call" | custom-call | tf_op jit(solution)/shard_map/pallas_call | solution.py:590
  60.5 2.1 %shard_map.162 = (f32[128,32,256]{2,1,0:T(8,128)}, f32[128,16,256]{2,1,0:T(8,128)S(1)}) custom-call(bf16[5120,256]{1,0:T(8,128)(2,1)S(1)} %get-tuple-element.52.field, bf16[128,192]{1,0:T(8,128)(2,1)S(1)} %get-tuple-element.53.wfin, bf16[1024,256]{1,0:T(8,128)(2,1)S(1)} %shard_map.161.shape, bf16[160,256]{1,0:T(8,128)(2,1)S(1)} %collective-permute-done.4.rxlo, ...), custom_call_target="tpu_custom_call" | custom-call | tf_op jit(solution)/shard_map/pallas_call | solution.py:499
  62.6 0.0 collective-permute-done.7.ryhi
  62.7 0.0 collective-permute-done.6.rylo
  62.7 1.6 %combine.1 = f32[128,32,256]{2,1,0:T(8,128)} custom-call(f32[128,32,256]{2,1,0:T(8,128)} %get-tuple-element.59.partial, f32[128,16,256]{2,1,0:T(8,128)S(1)} %get-tuple-element.60.rims, bf16[64,32]{1,0:T(8,128)(2,1)S(1)} %get-tuple-element.61.spread, bf16[512,256]{1,0:T(8,128)(2,1)S(1)} %collective-permute-done.6.rylo, ...), custom_call_target="tpu_custom_call", output_to_operand_aliasing={{}: (0, {})} | custom-call | tf_op jit(solution)/shard_map/combine/pallas_call | solution.py:539
  (10 shorter events, 0.1 us)
Async XLA Ops:
  0.0 6.6 %copy-start.3 = (f32[32,32]{1,0:T(8,128)S(1)}, f32[32,32]{1,0:T(8,128)}, u32[]{:S(2)}) copy-start(f32[32,32]{1,0:T(8,128)} %mode_x.1) | copy-start | bytes 12292
  0.0 6.6 %copy-start.5 = (bf16[256,4]{0,1:T(4,128)(2,1)S(1)}, bf16[256,4]{0,1:T(4,128)(2,1)}, u32[]{:S(2)}) copy-start(bf16[256,4]{0,1:T(4,128)(2,1)} %param.25) | copy-start | bytes 6148
  0.0 27.0 %copy-start = (bf16[256,256]{1,0:T(8,128)(2,1)S(1)}, bf16[256,256]{1,0:T(8,128)(2,1)}, u32[]{:S(2)}) copy-start(bf16[256,256]{1,0:T(8,128)(2,1)} %refs_2_.1) | copy-start | bytes 393220
  0.0 27.0 %copy-start.4 = (bf16[40,40]{1,0:T(8,128)(2,1)S(1)}, bf16[40,40]{1,0:T(8,128)(2,1)}, u32[]{:S(2)}) copy-start(bf16[40,40]{1,0:T(8,128)(2,1)} %refs_1_.1) | copy-start | bytes 9604
  0.0 27.0 %copy-start.1 = (bf16[136,136]{1,0:T(8,128)(2,1)S(1)}, bf16[136,136]{1,0:T(8,128)(2,1)}, u32[]{:S(2)}) copy-start(bf16[136,136]{1,0:T(8,128)(2,1)} %refs_0_.1) | copy-start | bytes 110980
  0.0 0.7 %copy-start.6 = (bf16[32,4]{0,1:T(4,128)(2,1)S(1)}, bf16[32,4]{0,1:T(4,128)(2,1)}, u32[]{:S(2)}) copy-start(bf16[32,4]{0,1:T(4,128)(2,1)} %param.24) | copy-start | bytes 772
  0.8 5.8 %copy-start.7 = (bf16[128,4]{0,1:T(4,128)(2,1)S(1)}, bf16[128,4]{0,1:T(4,128)(2,1)}, u32[]{:S(2)}) copy-start(bf16[128,4]{0,1:T(4,128)(2,1)} %param.23) | copy-start | bytes 3076
  0.8 5.8 %copy-start.8 = (f32[4,4]{1,0:T(4,128)S(1)}, f32[4,4]{1,0:T(4,128)}, u32[]{:S(2)}) copy-start(f32[4,4]{1,0:T(4,128)} %mode_z.1) | copy-start | bytes 196
  0.8 26.2 %copy-start.9 = (f32[136]{0:T(256)S(1)}, f32[136]{0:T(256)}, u32[]{:S(2)}) copy-start(f32[136]{0:T(256)} %param.20) | copy-start | bytes 1636
  0.8 26.3 %copy-start.10 = (f32[256]{0:T(256)S(1)}, f32[256]{0:T(256)}, u32[]{:S(2)}) copy-start(f32[256]{0:T(256)} %param.22) | copy-start | bytes 3076
  0.8 26.3 %copy-start.14 = (f32[40]{0:T(128)S(1)}, f32[40]{0:T(128)}, u32[]{:S(2)}) copy-start(f32[40]{0:T(128)} %param.21) | copy-start | bytes 484
  3.3 55.7 %copy-start.2 = (f32[128,128]{1,0:T(8,128)S(1)}, f32[128,128]{1,0:T(8,128)}, u32[]{:S(2)}) copy-start(f32[128,128]{1,0:T(8,128)} %mode_y.1) | copy-start | bytes 196612
  3.4 55.7 %copy-start.11 = (f32[32]{0:T(128)S(1)}, f32[32]{0:T(128)}, u32[]{:S(2)}) copy-start(f32[32]{0:T(128)} %param.29) | copy-start | bytes 388
  3.4 55.7 %copy-start.12 = (f32[128]{0:T(128)S(1)}, f32[128]{0:T(128)}, u32[]{:S(2)}) copy-start(f32[128]{0:T(128)} %param.30) | copy-start | bytes 1540
  3.4 55.7 %copy-start.13 = (f32[4]{0:T(128)S(1)}, f32[4]{0:T(128)}, u32[]{:S(2)}) copy-start(f32[4]{0:T(128)} %param.31) | copy-start | bytes 52
  3.4 4.0 %collective-permute-start = (bf16[128,256]{1,0:T(8,128)(2,1)S(1)}, bf16[128,256]{1,0:T(8,128)(2,1)S(1)}, u32[]{:S(2)}, u32[]{:S(2)}) collective-permute-start(bf16[128,256]{1,0:T(8,128)(2,1)S(1)} %get-tuple-element.34), channel_id=1, source_target_pairs={{0,32},{32,64},{64,96},{96,128},{128,160},{160,192},{192,224},{224... | collective-permute-start | bytes 196616 | tf_op jit(solution)/shard_map/ppermute | solution.py:553
  6.0 3.7 %collective-permute-start.1 = (bf16[128,256]{1,0:T(8,128)(2,1)S(1)}, bf16[128,256]{1,0:T(8,128)(2,1)S(1)}, u32[]{:S(2)}, u32[]{:S(2)}) collective-permute-start(bf16[128,256]{1,0:T(8,128)(2,1)S(1)} %get-tuple-element.35), channel_id=1, source_target_pairs={{0,224},{32,0},{64,32},{96,64},{128,96},{160,128},{192,160},{224,1... | collective-permute-start | bytes 196616 | tf_op jit(solution)/shard_map/ppermute | solution.py:553
  9.8 18.2 %collective-permute-start.2 = (bf16[544,256]{1,0:T(8,128)(2,1)S(1)}, bf16[544,256]{1,0:T(8,128)(2,1)S(1)}, u32[]{:S(2)}, u32[]{:S(2)}) collective-permute-start(bf16[544,256]{1,0:T(8,128)(2,1)S(1)} %get-tuple-element.41), channel_id=1, source_target_pairs={{0,1},{1,2},{2,3},{3,4},{4,5},{5,6},{6,7},{7,8},{8,9},{9,10},{10,1... | collective-permute-start | bytes 835592 | tf_op jit(solution)/shard_map/ppermute | solution.py:553
  11.2 16.9 %collective-permute-start.3 = (bf16[544,256]{1,0:T(8,128)(2,1)S(1)}, bf16[544,256]{1,0:T(8,128)(2,1)S(1)}, u32[]{:S(2)}, u32[]{:S(2)}) collective-permute-start(bf16[544,256]{1,0:T(8,128)(2,1)S(1)} %get-tuple-element.42), channel_id=1, source_target_pairs={{0,31},{1,0},{2,1},{3,2},{4,3},{5,4},{6,5},{7,6},{8,7},{9,8},{10,9... | collective-permute-start | bytes 835592 | tf_op jit(solution)/shard_map/ppermute | solution.py:553
  35.8 2.4 %collective-permute-start.4 = (bf16[160,256]{1,0:T(8,128)(2,1)S(1)}, bf16[160,256]{1,0:T(8,128)(2,1)S(1)}, u32[]{:S(2)}, u32[]{:S(2)}) collective-permute-start(bf16[160,256]{1,0:T(8,128)(2,1)S(1)} %get-tuple-element.56), channel_id=1, source_target_pairs={{0,32},{32,64},{64,96},{96,128},{128,160},{160,192},{192,224},{224... | collective-permute-start | bytes 245768 | tf_op jit(solution)/shard_map/ppermute | solution.py:553
  36.7 4.2 %collective-permute-start.5 = (bf16[160,256]{1,0:T(8,128)(2,1)S(1)}, bf16[160,256]{1,0:T(8,128)(2,1)S(1)}, u32[]{:S(2)}, u32[]{:S(2)}) collective-permute-start(bf16[160,256]{1,0:T(8,128)(2,1)S(1)} %get-tuple-element.57), channel_id=1, source_target_pairs={{0,224},{32,0},{64,32},{96,64},{128,96},{160,128},{192,160},{224,1... | collective-permute-start | bytes 245768 | tf_op jit(solution)/shard_map/ppermute | solution.py:553
  40.9 21.8 %collective-permute-start.7 = (bf16[512,256]{1,0:T(8,128)(2,1)S(1)}, bf16[512,256]{1,0:T(8,128)(2,1)S(1)}, u32[]{:S(2)}, u32[]{:S(2)}) collective-permute-start(bf16[512,256]{1,0:T(8,128)(2,1)S(1)} %get-tuple-element.62), channel_id=1, source_target_pairs={{0,31},{1,0},{2,1},{3,2},{4,3},{5,4},{6,5},{7,6},{8,7},{9,8},{10,9... | collective-permute-start | bytes 786440 | tf_op jit(solution)/shard_map/ppermute | solution.py:553
  42.3 20.3 %collective-permute-start.6 = (bf16[512,256]{1,0:T(8,128)(2,1)S(1)}, bf16[512,256]{1,0:T(8,128)(2,1)S(1)}, u32[]{:S(2)}, u32[]{:S(2)}) collective-permute-start(bf16[512,256]{1,0:T(8,128)(2,1)S(1)} %get-tuple-element.58.after), channel_id=1, source_target_pairs={{0,1},{1,2},{2,3},{3,4},{4,5},{5,6},{6,7},{7,8},{8,9},{9,10},{10,1... | collective-permute-start | bytes 786440 | tf_op jit(solution)/shard_map/ppermute | solution.py:553
where the time goes:
time: 64.4 us; the launch traced here: 64.3 us
  blocking collectives  25.4 us (39%)
  Pallas kernels  17.6 us (27%)
  starting transfers between devices  13.8 us (21%)
  waiting for transfers between devices  6.41 us (10%)
  local copies, waits for them, and re-layouts  0.8 us (1%)
    all_to_all x2, blocking collectives, exchange(): return lax.all_to_all(x, axis, 0, 0)  25.4 us
    ppermute x8, starting transfers between devices, shift(): return lax.ppermute(x, axis, [(i, (i + step) % size) for i in range(size)])  13.8 us
    pallas_call x1, Pallas kernels, solve(): call(solve_kernel, (sds((BLOCKS * ROWS, NZ), bf16), strip, strip, rim, ri...  7.73 us
    ppermute x8, waiting for transfers between devices, shift(): return lax.ppermute(x, axis, [(i, (i + step) % size) for i in range(size)])  6.41 us
    pallas_call x1, Pallas kernels, load(): call(load_kernel, (sds((OWN, NZ), bf16), sds((OWN, NZ), bf16), rim, rim,...  2.54 us
    pallas_call x1, Pallas kernels, finish(): call(finish_kernel, (sds((CX, CY, NZ), f32), sds((CX, 16, NZ), f32)), [VM...  2.11 us
    pallas_call x1, Pallas kernels, combine(): pl.pallas_call(combine_kernel, out_shape=sds((CX, CY, NZ), f32), in_specs...  1.61 us
    pallas_call x1, Pallas kernels, local(): call(coarse_kernel, sds((2 * CX * MODES, NZ), bf16), [VM] * 8 + [ANY], 8)  1.46 us
  transfers between devices with their start and end apart: 8, of which 3 were waited for; matrix products, arithmetic and copies ran while one was open for 0% of the time, Pallas kernels for 9%

commit v1 on v0

--- a/solution.py
+++ b/solution.py
@@ -154,7 +154,7 @@
             pltpu.VMEM((CELLS, NZ), f32), pltpu.SemaphoreType.DMA((CHUNKS,)),
             pltpu.VMEM((MODES, CY), bf16), pltpu.SemaphoreType.DMA,
         ],
-    )(residual, coarse_y.T)
+    )(residual, pltpu.with_memory_space_constraint(coarse_y.T, pltpu.HBM))
 
 
 def corners_kernel(sel, rim_lo, rim_hi, xlo, xhi, after, down, up):
@@ -210,17 +210,7 @@
 
 def prepare_kernel(*refs):
     n = len(PARAMS)
-    sources, outs, bufs, sems = (
-        refs[:n], refs[n + 1 : n + 1 + len(WEIGHTS)], refs[n + 1 + len(WEIGHTS) : -1], refs[-1]
-    )
-    copies = [
-        pltpu.make_async_copy(source, buf, sems.at[i])
-        for i, (source, buf) in enumerate(zip(sources, bufs))
-    ]
-    for copy in copies:
-        copy.start()
-    for copy in copies:
-        copy.wait()
+    bufs, outs = refs[:n], refs[n + 1 :]
     lx, ly, lz, eig_x, eig_y, eig_z, cyt = bufs
     wy, wyt, wfin, spread, wx, wxt, lz_out, lzt, exb, eyz = outs
 
@@ -278,11 +268,7 @@
 
 def prepare(*params):
     return call(
-        prepare_kernel,
-        tuple(sds(*w) for w in WEIGHTS),
-        [HBM] * len(PARAMS) + [ANY],
-        8,
-        scratch=[pltpu.VMEM(*p) for p in PARAMS] + [pltpu.SemaphoreType.DMA((len(PARAMS),))],
+        prepare_kernel, tuple(sds(*w) for w in WEIGHTS), [VM] * len(PARAMS) + [ANY], 8
     )(*params)
 
 
@@ -392,20 +378,15 @@
     )(*args)
 
 
-def fold_kernel(out_ylo, out_yhi, rxlo, rxhi, down, up):
-    end = CX * OV
-    for strip, start, out in ((out_ylo, OWN, down), (out_yhi, OWN + RIM, up)):
-        rows = slice(start, start + RIM)
-        out[...] = strip[...]
-        low = strip[:RIM, :].astype(f32) + rxlo[rows, :].astype(f32)
-        high = strip[end - RIM :, :].astype(f32) + rxhi[rows, :].astype(f32)
-        out[:RIM, :] = low.astype(bf16)
-        out[end - RIM :, :] = high.astype(bf16)
-
-
-def fold(*args):
-    rim = sds((CX * OV, NZ), bf16)
-    return call(fold_kernel, (rim, rim), [VM] * 4, 8)(*args)
+def turn_kernel(rxlo, rxhi, down, up):
+    for start, out in ((OWN, down), (OWN + RIM, up)):
+        out[:RIM, :] = rxlo[start : start + RIM, :]
+        out[RIM:, :] = rxhi[start : start + RIM, :]
+
+
+def turn(*args):
+    both = sds((2 * RIM, NZ), bf16)
+    return call(turn_kernel, (both, both), [VM] * 2, 4)(*args)
 
 
 def restrict_kernel(along_y, cxt, czt, mode_x, mode_z, out, modes_xz):
@@ -429,7 +410,24 @@
         out[i] = part
 
 
-def coarse_kernel(rows, modes_xz, mode_y, ceig_x, ceig_y, ceig_z, cxt, czt, after, out):
+COARSE = (
+    ((128, 128), f32), ((1, 32), f32), ((1, 128), f32), ((1, MODES), f32), ((MODES, CX), bf16),
+    ((MODES, NZ), bf16),
+)
+
+
+def coarse_kernel(rows, modes_xz, *refs):
+    n = len(COARSE)
+    sources, out, bufs, sems = refs[:n], refs[n + 1], refs[n + 2 : -1], refs[-1]
+    copies = [
+        pltpu.make_async_copy(source, buf, sems.at[i])
+        for i, (source, buf) in enumerate(zip(sources, bufs))
+    ]
+    for copy in copies:
+        copy.start()
+    for copy in copies:
+        copy.wait()
+    mode_y, ceig_x, ceig_y, ceig_z, cxt, czt = bufs
     to_a, to_c = modes_a()
     eight_x = jnp.broadcast_to(ceig_x[...], (8, 32))
     eight_z = jnp.broadcast_to(ceig_z[...], (8, MODES))
@@ -506,7 +504,7 @@
     )(*args)
 
 
-def combine_kernel(partial, rims, spread, rylo, ryhi, out, buf, sems):
+def combine_kernel(partial, rims, spread, rylo, ryhi, cornlo, cornhi, out, buf, sems):
     planes = CX // CHUNKS
     per = BLOCKS // CHUNKS
 
@@ -525,7 +523,12 @@
             k = c * per + b
             rim = slice(k * RIM, (k + 1) * RIM)
             data = jnp.concatenate([rylo[rim, :], ryhi[rim, :]], 0)
-            strips = dot(spread[...], data).reshape(GX, 16, NZ)
+            strips = dot(spread[...], data)
+            if k in (0, BLOCKS - 1):
+                at = slice(0, RIM) if k == 0 else slice(RIM, 2 * RIM)
+                data = jnp.concatenate([cornlo[at, :], cornhi[at, :]], 0)
+                strips = strips + dot(spread[...], data)
+            strips = strips.reshape(GX, 16, NZ)
             at = slice(k * GX, (k + 1) * GX)
             buf[at] = rims[at] + strips
         for copy in copies(c):
@@ -539,7 +542,7 @@
     return pl.pallas_call(
         combine_kernel,
         out_shape=sds((CX, CY, NZ), f32),
-        in_specs=[HBM] + [VM] * 4,
+        in_specs=[HBM] + [VM] * 6,
         out_specs=HBM,
         scratch_shapes=[pltpu.VMEM((CX, 16, NZ), f32), pltpu.SemaphoreType.DMA((2 * CHUNKS,))],
         input_output_aliases={0: 0},
@@ -582,17 +585,29 @@
         cells, xlo, xhi, ylo, yhi, wy, wyt, wx, wxt, lz, lzt, exb, eyz, part
     )
 
+    rylo = shift(out_yhi, "gy", 1)
+    ryhi = shift(out_ylo, "gy", -1)
     rxlo = shift(out_xhi, "gx", 1)
     rxhi = shift(out_xlo, "gx", -1)
-    down, up = fold(out_ylo, out_yhi, rxlo, rxhi)
-    rylo = shift(up, "gy", 1)
-    ryhi = shift(down, "gy", -1)
-    shape = call(coarse_kernel, sds((2 * CX * MODES, NZ), bf16), [VM] * 8 + [ANY], 8)(
-        rows, modes_xz, mode_y, coarse_eig_x[None], coarse_eig_y[None], coarse_eig_z[None],
-        coarse_x.T, coarse_z.T, up,
-    )
+    down, up = turn(rxlo, rxhi)
+    cornlo = shift(up, "gy", 1)
+    cornhi = shift(down, "gy", -1)
+    far = [
+        pltpu.with_memory_space_constraint(x, pltpu.HBM)
+        for x in (
+            mode_y, coarse_eig_x[None], coarse_eig_y[None], coarse_eig_z[None], coarse_x.T,
+            coarse_z.T,
+        )
+    ]
+    shape = call(
+        coarse_kernel,
+        sds((2 * CX * MODES, NZ), bf16),
+        [VM] * 2 + [HBM] * len(far) + [ANY],
+        8,
+        scratch=[pltpu.VMEM(*c) for c in COARSE] + [pltpu.SemaphoreType.DMA((len(COARSE),))],
+    )(rows, modes_xz, *far, out_ylo)
     partial, rims = finish(field, wfin, shape, rxlo, rxhi, up)
-    return combine(partial, rims, spread, rylo, ryhi)
+    return combine(partial, rims, spread, rylo, ryhi, cornlo, cornhi)
 
 
 def solution(mesh):

time: 64.4 us -> 68 us (1.056)
  blocking collectives: 25.4 us -> 8.78 us
  starting transfers between devices: 13.8 us -> 28.1 us
  Pallas kernels: 17.6 us -> 22.3 us
  waiting for transfers between devices: 6.41 us -> 8.23 us
  local copies, waits for them, and re-layouts: 0.8 us -> 0.05 us
    all_to_all x2 -> x1, blocking collectives: 25.4 us -> 8.78 us  [exchange(): return lax.all_to_all(x, axis, 0, 0)]
    ppermute x8 -> x10, starting transfers between devices: 13.8 us -> 22.9 us  [shift(): return lax.ppermute(x, axis, [(i, (i + step) % size) for i in range(size)])]
    all_to_all x0 -> x1, starting transfers between devices: none -> 5.25 us  [exchange(): return lax.all_to_all(x, axis, 0, 0)]
    ppermute x8 -> x10, waiting for transfers between devices: 6.41 us -> 8.23 us  [shift(): return lax.ppermute(x, axis, [(i, (i + step) % size) for i in range(size)])]
    pallas_call x1, Pallas kernels: 2.54 us -> 3.79 us  [load(): call(load_kernel, (sds((OWN, NZ), bf16), sds((OWN, NZ), bf16), rim, rim,...]
    pallas_call x3, Pallas kernels: 2.46 us -> 3.55 us  [the longest x1 2.37 us: local(): call(coarse_kernel, sds((2 * CX * MODES, NZ), bf16), [VM] * 2 + [HBM] * l...]
    pallas_call x1, Pallas kernels: 1.61 us -> 2.57 us  [combine(): pl.pallas_call(combine_kernel, out_shape=sds((CX, CY, NZ), f32), in_specs...]
    unnamed x30 -> x24, local copies, waits for them, and re-layouts: 0.8 us -> 0.05 us
  transfers between devices with their start and end apart: 8 -> 11, of which waited for: 3 -> 4; matrix products, arithmetic and copies ran while one was open for 0% -> 0% of each run, Pallas kernels for 9% -> 11%
where the time goes in v1:
time: 68 us; the launch traced here: 67.7 us
  starting transfers between devices  28.1 us (41%)
  Pallas kernels  22.3 us (33%)
  blocking collectives  8.78 us (13%)
  waiting for transfers between devices  8.23 us (12%)
    ppermute x10, starting transfers between devices, shift(): return lax.ppermute(x, axis, [(i, (i + step) % size) for i in range(size)])  22.9 us
    all_to_all x1, blocking collectives, exchange(): return lax.all_to_all(x, axis, 0, 0)  8.78 us
    pallas_call x1, Pallas kernels, solve(): call(solve_kernel, (sds((BLOCKS * ROWS, NZ), bf16), strip, strip, rim, ri...  8.46 us
    ppermute x10, waiting for transfers between devices, shift(): return lax.ppermute(x, axis, [(i, (i + step) % size) for i in range(size)])  8.23 us
    all_to_all x1, starting transfers between devices, exchange(): return lax.all_to_all(x, axis, 0, 0)  5.25 us
    pallas_call x1, Pallas kernels, load(): call(load_kernel, (sds((OWN, NZ), bf16), sds((OWN, NZ), bf16), rim, rim,...  3.79 us
    pallas_call x1, Pallas kernels, combine(): pl.pallas_call(combine_kernel, out_shape=sds((CX, CY, NZ), f32), in_specs...  2.57 us
    pallas_call x1, Pallas kernels, local(): call(coarse_kernel, sds((2 * CX * MODES, NZ), bf16), [VM] * 2 + [HBM] * l...  2.37 us
  transfers between devices with their start and end apart: 11, of which 4 were waited for; matrix products, arithmetic and copies ran while one was open for 0% of the time, Pallas kernels for 11%

profile of v1, /device:TPU:1, one launch (start us, length us, event | category | flops | bytes accessed | tf_op | source)
XLA Modules:
  0.0 67.7 jit_solution(10200098470786874860)
XLA Ops:
  0.0 0.0 copy-start.4
  0.0 0.0 copy-start.6
  0.0 0.0 copy-start.9
  0.0 0.0 copy-start.10
  0.1 0.0 copy-start.8
  0.1 0.0 copy-start
  0.1 0.0 copy-start.3
  0.1 0.0 copy-start.1
  0.1 3.8 %shard_map.154 = (bf16[128,256]{1,0:T(8,128)(2,1)S(1)}, bf16[128,256]{1,0:T(8,128)(2,1)S(1)}, bf16[512,256]{1,0:T(8,128)(2,1)S(1)}, bf16[512,256]{1,0:T(8,128)(2...) custom-call(f32[4096,256]{1,0:T(8,128)} %bitcast.19, bf16[4,32]{1,0:T(4,128)(2,1)} %bitcast.12), custom_call_target="tpu_custom_call" | custom-call | tf_op jit(solution)/shard_map/pallas_call | solution.py:145
  3.9 2.6 %collective-permute-start = (bf16[128,256]{1,0:T(8,128)(2,1)S(1)}, bf16[128,256]{1,0:T(8,128)(2,1)S(1)}, u32[]{:S(2)}, u32[]{:S(2)}) collective-permute-start(bf16[128,256]{1,0:T(8,128)(2,1)S(1)} %get-tuple-element.34), channel_id=1, source_target_pairs={{0,32},{32,64},{64,96},{96,128},{128,160},{160,192},{192,224},{224... | collective-permute-start | bytes 196616 | tf_op jit(solution)/shard_map/ppermute | solution.py:556
  6.5 0.6 collective-permute-start.1
  7.1 0.0 copy-done.7
  7.1 0.0 copy-done.6
  7.1 0.8 %shard_map.155 = (f32[8,4,16]{2,1,0:T(4,128)S(1)}, f32[128,128]{1,0:T(8,128)S(1)}) custom-call(f32[512,256]{1,0:T(8,128)S(1)} %get-tuple-element.39.along_y, bf16[4,128]{1,0:T(4,128)(2,1)S(1)} %bitcast.15, bf16[4,256]{1,0:T(4,128)(2,1)S(1)} %bitcast.11, f32[32,32]{1,0:T(8,128)S(1)} %copy-done.2, f32[4,4]{1,0:T(4,128)S(1)} %copy-done.7), custom_call_target="tpu_custom_call" | custom-call | tf_op jit(solution)/shard_map/pallas_call | solution.py:571
  8.0 0.0 collective-permute-done.xlo
  8.0 2.2 %collective-permute-done.1.xhi = bf16[128,256]{1,0:T(8,128)(2,1)S(1)} collective-permute-done((bf16[128,256]{1,0:T(8,128)(2,1)S(1)}, bf16[128,256]{1,0:T(8,128)(2,1)S(1)}, u32[]{:S(2)}, u32[]{:S(2)}) %collective-permute-start.1) | collective-permute-done | bytes 65568 | tf_op jit(solution)/shard_map/ppermute | solution.py:556
  10.2 0.1 shard_map.156
  10.3 1.3 %collective-permute-start.2 = (bf16[544,256]{1,0:T(8,128)(2,1)S(1)}, bf16[544,256]{1,0:T(8,128)(2,1)S(1)}, u32[]{:S(2)}, u32[]{:S(2)}) collective-permute-start(bf16[544,256]{1,0:T(8,128)(2,1)S(1)} %get-tuple-element.41), channel_id=1, source_target_pairs={{0,1},{1,2},{2,3},{3,4},{4,5},{5,6},{6,7},{7,8},{8,9},{9,10},{10,1... | collective-permute-start | bytes 835592 | tf_op jit(solution)/shard_map/ppermute | solution.py:556
  11.7 6.8 %collective-permute-start.3 = (bf16[544,256]{1,0:T(8,128)(2,1)S(1)}, bf16[544,256]{1,0:T(8,128)(2,1)S(1)}, u32[]{:S(2)}, u32[]{:S(2)}) collective-permute-start(bf16[544,256]{1,0:T(8,128)(2,1)S(1)} %get-tuple-element.42), channel_id=1, source_target_pairs={{0,31},{1,0},{2,1},{3,2},{4,3},{5,4},{6,5},{7,6},{8,7},{9,8},{10,9... | collective-permute-start | bytes 835592 | tf_op jit(solution)/shard_map/ppermute | solution.py:556
  18.5 8.8 %all_to_all.10.rows = f32[8,4,16]{2,1,0:T(4,128)S(1)} all-to-all(f32[8,4,16]{2,1,0:T(4,128)S(1)} %get-tuple-element.40.after), channel_id=1, replica_groups=mesh['gx'=8,'gy'=32] {'gx'}, dimensions={0} | all-to-all | bytes 4096 | tf_op jit(solution)/shard_map/all_to_all | solution.py:560
  27.3 0.9 %shard_map.157.refs_7_.after = f32[32,4,128]{2,1,0:T(4,128)} custom-call(f32[8,4,16]{2,1,0:T(4,128)S(1)} %all_to_all.10.rows, f32[128,128]{1,0:T(8,128)S(1)} %get-tuple-element.43.modes_xz), custom_call_target="tpu_custom_call" | custom-call | tf_op jit(solution)/shard_map/pallas_call | solution.py:578
  28.1 0.0 copy-done.8
  28.1 0.0 copy-done
  28.1 0.0 copy-done.3
  28.1 0.0 copy-done.1
  28.1 0.6 shard_map.158
  28.7 0.0 collective-permute-done.2.ylo
  28.7 0.0 collective-permute-done.3.yhi
  28.8 8.5 %shard_map.159 = (bf16[5120,256]{1,0:T(8,128)(2,1)S(1)}, bf16[160,256]{1,0:T(8,128)(2,1)S(1)}, bf16[160,256]{1,0:T(8,128)(2,1)}, bf16[512,256]{1,0:T(8,128)(2,1)S(1)}, bf16[512,256]{1,0:T(8,128)(2,1)}) custom-call(f32[4096,256]{1,0:T(8,128)} %bitcast.20, bf16[128,256]{1,0:T(8,128)(2,1)S(1)} %collective-permute-done.xlo, ...), custom_call_target="tpu_custom_call" | custom-call | tf_op jit(solution)/shard_map/pallas_call | solution.py:368
  37.2 0.1 collective-permute-start.6
  37.3 4.8 %collective-permute-start.7 = (bf16[512,256]{1,0:T(8,128)(2,1)S(1)}, bf16[512,256]{1,0:T(8,128)(2,1)}, u32[]{:S(2)}, u32[]{:S(2)}) collective-permute-start(bf16[512,256]{1,0:T(8,128)(2,1)S(1)} %get-tuple-element.54.refs_6_), channel_id=1, source_target_pairs={{0,31},{1,0},{2,1},{3,2},{4,3},{5,4},{6,5},{7,6},{8,7},{9,8},{10,9... | collective-permute-start | bytes 786440 | tf_op jit(solution)/shard_map/ppermute | solution.py:556
  42.1 5.2 %all-to-all-start.1 = ((f32[32,4,128]{2,1,0:T(4,128)}), f32[32,4,128]{2,1,0:T(4,128)S(1)}, u32[]{:S(2)}, u32[]{:S(2)}) async-start(f32[32,4,128]{2,1,0:T(4,128)} %shard_map.157.refs_7_.after), calls=%async_computation.1 | async-start | bytes 131072 | tf_op jit(solution)/shard_map/all_to_all | solution.py:560
  47.3 0.0 copy-done.11
  47.4 1.7 %collective-permute-start.4 = (bf16[160,256]{1,0:T(8,128)(2,1)}, bf16[160,256]{1,0:T(8,128)(2,1)S(1)}, u32[]{:S(2)}, u32[]{:S(2)}) collective-permute-start(bf16[160,256]{1,0:T(8,128)(2,1)} %get-tuple-element.55), channel_id=1, source_target_pairs={{0,32},{32,64},{64,96},{96,128},{128,160},{160,192},{192,224},{224... | collective-permute-start | bytes 245768 | tf_op jit(solution)/shard_map/ppermute | solution.py:556
  49.1 0.0 collective-permute-start.5
  49.1 1.8 %collective-permute-done.4.rxlo = bf16[160,256]{1,0:T(8,128)(2,1)S(1)} collective-permute-done((bf16[160,256]{1,0:T(8,128)(2,1)}, bf16[160,256]{1,0:T(8,128)(2,1)S(1)}, u32[]{:S(2)}, u32[]{:S(2)}) %collective-permute-start.4) | collective-permute-done | bytes 81952 | tf_op jit(solution)/shard_map/ppermute | solution.py:556
  50.9 2.6 %collective-permute-done.5.rxhi = bf16[160,256]{1,0:T(8,128)(2,1)S(1)} collective-permute-done((bf16[160,256]{1,0:T(8,128)(2,1)}, bf16[160,256]{1,0:T(8,128)(2,1)S(1)}, u32[]{:S(2)}, u32[]{:S(2)}) %collective-permute-start.5) | collective-permute-done | bytes 81952 | tf_op jit(solution)/shard_map/ppermute | solution.py:556
  53.4 0.6 shard_map.161
  54.1 4.9 %collective-permute-start.9 = (bf16[32,256]{1,0:T(8,128)(2,1)}, bf16[32,256]{1,0:T(8,128)(2,1)S(1)}, u32[]{:S(2)}, u32[]{:S(2)}) collective-permute-start(bf16[32,256]{1,0:T(8,128)(2,1)} %get-tuple-element.62), channel_id=1, source_target_pairs={{0,31},{1,0},{2,1},{3,2},{4,3},{5,4},{6,5},{7,6},{8,7},{9,8},{10,9... | collective-permute-start | bytes 49160 | tf_op jit(solution)/shard_map/ppermute | solution.py:556
  59.0 0.0 collective-permute-start.8
  59.0 0.0 all-to-all-done.1.rows
  59.0 2.4 %shard_map.160.shape = bf16[1024,256]{1,0:T(8,128)(2,1)S(1)} custom-call(f32[32,4,128]{2,1,0:T(4,128)S(1)} %all-to-all-done.1.rows, f32[128,128]{1,0:T(8,128)S(1)} %get-tuple-element.43.modes_xz, f32[128,128]{1,0:T(8,128)} %refs_0_.3, f32[1,32]{1,0:T(1,128)} %bitcast.21, f32[1,128]{1,0:T(1,128)} %bitcast.22, f32[1,4]{1,0:T(1,128)} %bitcast.23, ...), custom_call_target="tpu_custom_call" | custom-call | tf_op jit(solution)/shard_map/pallas_call | solution.py:602
  61.4 2.1 %shard_map.162 = (f32[128,32,256]{2,1,0:T(8,128)}, f32[128,16,256]{2,1,0:T(8,128)S(1)}) custom-call(bf16[5120,256]{1,0:T(8,128)(2,1)S(1)} %get-tuple-element.52.field, bf16[128,192]{1,0:T(8,128)(2,1)S(1)} %get-tuple-element.53.wfin, bf16[1024,256]{1,0:T(8,128)(2,1)S(1)} %shard_map.160.shape, bf16[160,256]{1,0:T(8,128)(2,1)S(1)} %collective-permute-done.4.rxlo, ...), custom_call_target="tpu_custom_call" | custom-call | tf_op jit(solution)/shard_map/pallas_call | solution.py:497
  63.4 0.0 collective-permute-done.9.cornhi
  63.5 1.6 %collective-permute-done.8.cornlo = bf16[32,256]{1,0:T(8,128)(2,1)S(1)} collective-permute-done((bf16[32,256]{1,0:T(8,128)(2,1)}, bf16[32,256]{1,0:T(8,128)(2,1)S(1)}, u32[]{:S(2)}, u32[]{:S(2)}) %collective-permute-start.8) | collective-permute-done | bytes 16416 | tf_op jit(solution)/shard_map/ppermute | solution.py:556
  65.1 0.0 collective-permute-done.6.rylo
  65.1 0.0 collective-permute-done.7.ryhi
  65.1 2.6 %combine.1 = f32[128,32,256]{2,1,0:T(8,128)} custom-call(f32[128,32,256]{2,1,0:T(8,128)} %get-tuple-element.58.partial, f32[128,16,256]{2,1,0:T(8,128)S(1)} %get-tuple-element.59.rims, bf16[64,32]{1,0:T(8,128)(2,1)S(1)} %get-tuple-element.60.spread, bf16[512,256]{1,0:T(8,128)(2,1)S(1)} %collective-permute-done.6.rylo, ...), custom_call_target="tpu_custom_call", output_to_operand_aliasing={{}: (0, {})} | custom-call | tf_op jit(solution)/shard_map/combine/pallas_call | solution.py:542
  (9 shorter events, 0.0 us)
Async XLA Ops:
  0.0 28.1 %copy-start.5 = (bf16[32,4]{0,1:T(4,128)(2,1)S(1)}, bf16[32,4]{0,1:T(4,128)(2,1)}, u32[]{:S(2)}) copy-start(bf16[32,4]{0,1:T(4,128)(2,1)} %param.24) | copy-start | bytes 772
  0.0 7.1 %copy-start.7 = (f32[4,4]{1,0:T(4,128)S(1)}, f32[4,4]{1,0:T(4,128)}, u32[]{:S(2)}) copy-start(f32[4,4]{1,0:T(4,128)} %mode_z.1) | copy-start | bytes 196
  0.0 7.1 %copy-start.2 = (f32[32,32]{1,0:T(8,128)S(1)}, f32[32,32]{1,0:T(8,128)}, u32[]{:S(2)}) copy-start(f32[32,32]{1,0:T(8,128)} %mode_x.1) | copy-start | bytes 12292
  0.0 7.1 %copy-start.4 = (bf16[256,4]{0,1:T(4,128)(2,1)S(1)}, bf16[256,4]{0,1:T(4,128)(2,1)}, u32[]{:S(2)}) copy-start(bf16[256,4]{0,1:T(4,128)(2,1)} %param.25) | copy-start | bytes 6148
  0.0 7.1 %copy-start.6 = (bf16[128,4]{0,1:T(4,128)(2,1)S(1)}, bf16[128,4]{0,1:T(4,128)(2,1)}, u32[]{:S(2)}) copy-start(bf16[128,4]{0,1:T(4,128)(2,1)} %param.23) | copy-start | bytes 3076
  0.0 28.1 %copy-start.9 = (f32[256]{0:T(256)S(1)}, f32[256]{0:T(256)}, u32[]{:S(2)}) copy-start(f32[256]{0:T(256)} %param.22) | copy-start | bytes 3076
  0.0 28.1 %copy-start.10 = (f32[40]{0:T(128)S(1)}, f32[40]{0:T(128)}, u32[]{:S(2)}) copy-start(f32[40]{0:T(128)} %param.21) | copy-start | bytes 484
  0.1 28.1 %copy-start.8 = (f32[136]{0:T(256)S(1)}, f32[136]{0:T(256)}, u32[]{:S(2)}) copy-start(f32[136]{0:T(256)} %param.20) | copy-start | bytes 1636
  0.1 28.1 %copy-start = (bf16[256,256]{1,0:T(8,128)(2,1)S(1)}, bf16[256,256]{1,0:T(8,128)(2,1)}, u32[]{:S(2)}) copy-start(bf16[256,256]{1,0:T(8,128)(2,1)} %refs_2_.1) | copy-start | bytes 393220
  0.1 28.1 %copy-start.3 = (bf16[40,40]{1,0:T(8,128)(2,1)S(1)}, bf16[40,40]{1,0:T(8,128)(2,1)}, u32[]{:S(2)}) copy-start(bf16[40,40]{1,0:T(8,128)(2,1)} %refs_1_.1) | copy-start | bytes 9604
  0.1 28.1 %copy-start.1 = (bf16[136,136]{1,0:T(8,128)(2,1)S(1)}, bf16[136,136]{1,0:T(8,128)(2,1)}, u32[]{:S(2)}) copy-start(bf16[136,136]{1,0:T(8,128)(2,1)} %refs_0_.2) | copy-start | bytes 110980
  3.9 4.1 %collective-permute-start = (bf16[128,256]{1,0:T(8,128)(2,1)S(1)}, bf16[128,256]{1,0:T(8,128)(2,1)S(1)}, u32[]{:S(2)}, u32[]{:S(2)}) collective-permute-start(bf16[128,256]{1,0:T(8,128)(2,1)S(1)} %get-tuple-element.34), channel_id=1, source_target_pairs={{0,32},{32,64},{64,96},{96,128},{128,160},{160,192},{192,224},{224... | collective-permute-start | bytes 196616 | tf_op jit(solution)/shard_map/ppermute | solution.py:556
  6.5 3.7 %collective-permute-start.1 = (bf16[128,256]{1,0:T(8,128)(2,1)S(1)}, bf16[128,256]{1,0:T(8,128)(2,1)S(1)}, u32[]{:S(2)}, u32[]{:S(2)}) collective-permute-start(bf16[128,256]{1,0:T(8,128)(2,1)S(1)} %get-tuple-element.35), channel_id=1, source_target_pairs={{0,224},{32,0},{64,32},{96,64},{128,96},{160,128},{192,160},{224,1... | collective-permute-start | bytes 196616 | tf_op jit(solution)/shard_map/ppermute | solution.py:556
  10.3 18.4 %collective-permute-start.2 = (bf16[544,256]{1,0:T(8,128)(2,1)S(1)}, bf16[544,256]{1,0:T(8,128)(2,1)S(1)}, u32[]{:S(2)}, u32[]{:S(2)}) collective-permute-start(bf16[544,256]{1,0:T(8,128)(2,1)S(1)} %get-tuple-element.41), channel_id=1, source_target_pairs={{0,1},{1,2},{2,3},{3,4},{4,5},{5,6},{6,7},{7,8},{8,9},{9,10},{10,1... | collective-permute-start | bytes 835592 | tf_op jit(solution)/shard_map/ppermute | solution.py:556
  11.7 17.1 %collective-permute-start.3 = (bf16[544,256]{1,0:T(8,128)(2,1)S(1)}, bf16[544,256]{1,0:T(8,128)(2,1)S(1)}, u32[]{:S(2)}, u32[]{:S(2)}) collective-permute-start(bf16[544,256]{1,0:T(8,128)(2,1)S(1)} %get-tuple-element.42), channel_id=1, source_target_pairs={{0,31},{1,0},{2,1},{3,2},{4,3},{5,4},{6,5},{7,6},{8,7},{9,8},{10,9... | collective-permute-start | bytes 835592 | tf_op jit(solution)/shard_map/ppermute | solution.py:556
  37.2 10.1 %copy-start.11 = (bf16[160,256]{1,0:T(8,128)(2,1)}, bf16[160,256]{1,0:T(8,128)(2,1)S(1)}, u32[]{:S(2)}) copy-start(bf16[160,256]{1,0:T(8,128)(2,1)S(1)} %get-tuple-element.56) | copy-start | bytes 245764
  37.2 27.9 %collective-permute-start.6 = (bf16[512,256]{1,0:T(8,128)(2,1)}, bf16[512,256]{1,0:T(8,128)(2,1)S(1)}, u32[]{:S(2)}, u32[]{:S(2)}) collective-permute-start(bf16[512,256]{1,0:T(8,128)(2,1)} %get-tuple-element.61), channel_id=1, source_target_pairs={{0,1},{1,2},{2,3},{3,4},{4,5},{5,6},{6,7},{7,8},{8,9},{9,10},{10,1... | collective-permute-start | bytes 786440 | tf_op jit(solution)/shard_map/ppermute | solution.py:556
  37.3 27.8 %collective-permute-start.7 = (bf16[512,256]{1,0:T(8,128)(2,1)S(1)}, bf16[512,256]{1,0:T(8,128)(2,1)}, u32[]{:S(2)}, u32[]{:S(2)}) collective-permute-start(bf16[512,256]{1,0:T(8,128)(2,1)S(1)} %get-tuple-element.54.refs_6_), channel_id=1, source_target_pairs={{0,31},{1,0},{2,1},{3,2},{4,3},{5,4},{6,5},{7,6},{8,7},{9,8},{10,9... | collective-permute-start | bytes 786440 | tf_op jit(solution)/shard_map/ppermute | solution.py:556
  42.1 16.9 %all-to-all-start.1 = ((f32[32,4,128]{2,1,0:T(4,128)}), f32[32,4,128]{2,1,0:T(4,128)S(1)}, u32[]{:S(2)}, u32[]{:S(2)}) async-start(f32[32,4,128]{2,1,0:T(4,128)} %shard_map.157.refs_7_.after), calls=%async_computation.1 | async-start | bytes 131072 | tf_op jit(solution)/shard_map/all_to_all | solution.py:560
  47.4 3.5 %collective-permute-start.4 = (bf16[160,256]{1,0:T(8,128)(2,1)}, bf16[160,256]{1,0:T(8,128)(2,1)S(1)}, u32[]{:S(2)}, u32[]{:S(2)}) collective-permute-start(bf16[160,256]{1,0:T(8,128)(2,1)} %get-tuple-element.55), channel_id=1, source_target_pairs={{0,32},{32,64},{64,96},{96,128},{128,160},{160,192},{192,224},{224... | collective-permute-start | bytes 245768 | tf_op jit(solution)/shard_map/ppermute | solution.py:556
  49.1 4.4 %collective-permute-start.5 = (bf16[160,256]{1,0:T(8,128)(2,1)}, bf16[160,256]{1,0:T(8,128)(2,1)S(1)}, u32[]{:S(2)}, u32[]{:S(2)}) collective-permute-start(bf16[160,256]{1,0:T(8,128)(2,1)} %copy-done.11), channel_id=1, source_target_pairs={{0,224},{32,0},{64,32},{96,64},{128,96},{160,128},{192,160},{224,1... | collective-permute-start | bytes 245768 | tf_op jit(solution)/shard_map/ppermute | solution.py:556
  54.1 9.4 %collective-permute-start.9 = (bf16[32,256]{1,0:T(8,128)(2,1)}, bf16[32,256]{1,0:T(8,128)(2,1)S(1)}, u32[]{:S(2)}, u32[]{:S(2)}) collective-permute-start(bf16[32,256]{1,0:T(8,128)(2,1)} %get-tuple-element.62), channel_id=1, source_target_pairs={{0,31},{1,0},{2,1},{3,2},{4,3},{5,4},{6,5},{7,6},{8,7},{9,8},{10,9... | collective-permute-start | bytes 49160 | tf_op jit(solution)/shard_map/ppermute | solution.py:556
  59.0 6.1 %collective-permute-start.8 = (bf16[32,256]{1,0:T(8,128)(2,1)}, bf16[32,256]{1,0:T(8,128)(2,1)S(1)}, u32[]{:S(2)}, u32[]{:S(2)}) collective-permute-start(bf16[32,256]{1,0:T(8,128)(2,1)} %get-tuple-element.57.after), channel_id=1, source_target_pairs={{0,1},{1,2},{2,3},{3,4},{4,5},{5,6},{6,7},{7,8},{8,9},{9,10},{10,1... | collective-permute-start | bytes 49160 | tf_op jit(solution)/shard_map/ppermute | solution.py:556

commit v2 on v1

--- a/solution.py
+++ b/solution.py
@@ -117,10 +117,10 @@
         at = pl.ds(c * rows, rows)
         return pltpu.make_async_copy(residual.at[at, :], buf.at[at, :], sems.at[c])
 
+    small = pltpu.make_async_copy(cyt, cyt_buf, sem)
+    small.start()
     for c in range(CHUNKS):
         copy(c).start()
-    small = pltpu.make_async_copy(cyt, cyt_buf, sem)
-    small.start()
     small.wait()
     take = selection(cyt_buf[...])
     sel[...] = take
@@ -378,7 +378,7 @@
     )(*args)
 
 
-def turn_kernel(rxlo, rxhi, down, up):
+def turn_kernel(rxlo, rxhi, after, down, up):
     for start, out in ((OWN, down), (OWN + RIM, up)):
         out[:RIM, :] = rxlo[start : start + RIM, :]
         out[RIM:, :] = rxhi[start : start + RIM, :]
@@ -386,7 +386,7 @@
 
 def turn(*args):
     both = sds((2 * RIM, NZ), bf16)
-    return call(turn_kernel, (both, both), [VM] * 2, 4)(*args)
+    return call(turn_kernel, (both, both), [VM] * 2 + [ANY], 4)(*args)
 
 
 def restrict_kernel(along_y, cxt, czt, mode_x, mode_z, out, modes_xz):
@@ -589,9 +589,6 @@
     ryhi = shift(out_ylo, "gy", -1)
     rxlo = shift(out_xhi, "gx", 1)
     rxhi = shift(out_xlo, "gx", -1)
-    down, up = turn(rxlo, rxhi)
-    cornlo = shift(up, "gy", 1)
-    cornhi = shift(down, "gy", -1)
     far = [
         pltpu.with_memory_space_constraint(x, pltpu.HBM)
         for x in (
@@ -606,6 +603,9 @@
         8,
         scratch=[pltpu.VMEM(*c) for c in COARSE] + [pltpu.SemaphoreType.DMA((len(COARSE),))],
     )(rows, modes_xz, *far, out_ylo)
+    down, up = turn(rxlo, rxhi, shape)
+    cornlo = shift(up, "gy", 1)
+    cornhi = shift(down, "gy", -1)
     partial, rims = finish(field, wfin, shape, rxlo, rxhi, up)
     return combine(partial, rims, spread, rylo, ryhi, cornlo, cornhi)
 

time: 68 us -> 70.1 us (1.031)
  the two profiles are of different devices: /device:TPU:1 before, /device:TPU:2 now
where the time goes in v2:
time: 70.1 us; the launch traced here: 69.8 us
  starting transfers between devices  25 us (36%)
  Pallas kernels  21.5 us (31%)
  waiting for transfers between devices  13.7 us (20%)
  blocking collectives  9.38 us (13%)
    ppermute x10, starting transfers between devices, shift(): return lax.ppermute(x, axis, [(i, (i + step) % size) for i in range(size)])  19.5 us
    all_to_all x1, blocking collectives, exchange(): return lax.all_to_all(x, axis, 0, 0)  9.38 us
    pallas_call x1, Pallas kernels, solve(): call(solve_kernel, (sds((BLOCKS * ROWS, NZ), bf16), strip, strip, rim, ri...  8.46 us
    all_to_all x1, waiting for transfers between devices, exchange(): return lax.all_to_all(x, axis, 0, 0)  8.22 us
    all_to_all x1, starting transfers between devices, exchange(): return lax.all_to_all(x, axis, 0, 0)  5.53 us
    ppermute x10, waiting for transfers between devices, shift(): return lax.ppermute(x, axis, [(i, (i + step) % size) for i in range(size)])  5.48 us
    pallas_call x1, Pallas kernels, load(): call(load_kernel, (sds((OWN, NZ), bf16), sds((OWN, NZ), bf16), rim, rim,...  3.63 us
    pallas_call x1, Pallas kernels, combine(): pl.pallas_call(combine_kernel, out_shape=sds((CX, CY, NZ), f32), in_specs...  2.57 us
  transfers between devices with their start and end apart: 11, of which 3 were waited for; matrix products, arithmetic and copies ran while one was open for 0% of the time, Pallas kernels for 10%

profile of v2, /device:TPU:2, one launch (start us, length us, event | category | flops | bytes accessed | tf_op | source)
XLA Modules:
  0.0 69.8 jit_solution(9632707272592967571)
XLA Ops:
  0.0 0.0 copy-start.4
  0.0 0.0 copy-start.6
  0.0 0.0 copy-start.9
  0.0 0.0 copy-start.10
  0.1 0.0 copy-start.8
  0.1 0.0 copy-start
  0.1 0.0 copy-start.3
  0.1 0.0 copy-start.1
  0.1 3.6 %shard_map.154 = (bf16[128,256]{1,0:T(8,128)(2,1)S(1)}, bf16[128,256]{1,0:T(8,128)(2,1)S(1)}, bf16[512,256]{1,0:T(8,128)(2,1)S(1)}, bf16[512,256]{1,0:T(8,128)(2...) custom-call(f32[4096,256]{1,0:T(8,128)} %bitcast.19, bf16[4,32]{1,0:T(4,128)(2,1)} %bitcast.12), custom_call_target="tpu_custom_call" | custom-call | tf_op jit(solution)/shard_map/pallas_call | solution.py:145
  3.7 0.0 collective-permute-start
  3.8 1.7 %collective-permute-start.1 = (bf16[128,256]{1,0:T(8,128)(2,1)S(1)}, bf16[128,256]{1,0:T(8,128)(2,1)S(1)}, u32[]{:S(2)}, u32[]{:S(2)}) collective-permute-start(bf16[128,256]{1,0:T(8,128)(2,1)S(1)} %get-tuple-element.35), channel_id=1, source_target_pairs={{0,224},{32,0},{64,32},{96,64},{128,96},{160,128},{192,160},{224,1... | collective-permute-start | bytes 196616 | tf_op jit(solution)/shard_map/ppermute | solution.py:556
  5.5 0.0 copy-done.7
  5.5 0.0 copy-done.2
  5.5 0.0 copy-done.4
  5.5 0.0 copy-done.6
  5.5 0.8 %shard_map.155 = (f32[8,4,16]{2,1,0:T(4,128)S(1)}, f32[128,128]{1,0:T(8,128)S(1)}) custom-call(f32[512,256]{1,0:T(8,128)S(1)} %get-tuple-element.39.along_y, bf16[4,128]{1,0:T(4,128)(2,1)S(1)} %bitcast.15, bf16[4,256]{1,0:T(4,128)(2,1)S(1)} %bitcast.11, f32[32,32]{1,0:T(8,128)S(1)} %copy-done.2, f32[4,4]{1,0:T(4,128)S(1)} %copy-done.7), custom_call_target="tpu_custom_call" | custom-call | tf_op jit(solution)/shard_map/pallas_call | solution.py:571
  6.3 1.1 %collective-permute-done.xlo = bf16[128,256]{1,0:T(8,128)(2,1)S(1)} collective-permute-done((bf16[128,256]{1,0:T(8,128)(2,1)S(1)}, bf16[128,256]{1,0:T(8,128)(2,1)S(1)}, u32[]{:S(2)}, u32[]{:S(2)}) %collective-permute-start) | collective-permute-done | bytes 65568 | tf_op jit(solution)/shard_map/ppermute | solution.py:556
  7.4 0.0 collective-permute-done.1.xhi
  7.4 0.1 shard_map.156
  7.6 1.6 %collective-permute-start.2 = (bf16[544,256]{1,0:T(8,128)(2,1)S(1)}, bf16[544,256]{1,0:T(8,128)(2,1)S(1)}, u32[]{:S(2)}, u32[]{:S(2)}) collective-permute-start(bf16[544,256]{1,0:T(8,128)(2,1)S(1)} %get-tuple-element.41), channel_id=1, source_target_pairs={{0,1},{1,2},{2,3},{3,4},{4,5},{5,6},{6,7},{7,8},{8,9},{9,10},{10,1... | collective-permute-start | bytes 835592 | tf_op jit(solution)/shard_map/ppermute | solution.py:556
  9.2 6.8 %collective-permute-start.3 = (bf16[544,256]{1,0:T(8,128)(2,1)S(1)}, bf16[544,256]{1,0:T(8,128)(2,1)S(1)}, u32[]{:S(2)}, u32[]{:S(2)}) collective-permute-start(bf16[544,256]{1,0:T(8,128)(2,1)S(1)} %get-tuple-element.42), channel_id=1, source_target_pairs={{0,31},{1,0},{2,1},{3,2},{4,3},{5,4},{6,5},{7,6},{8,7},{9,8},{10,9... | collective-permute-start | bytes 835592 | tf_op jit(solution)/shard_map/ppermute | solution.py:556
  16.0 9.4 %all_to_all.10.rows = f32[8,4,16]{2,1,0:T(4,128)S(1)} all-to-all(f32[8,4,16]{2,1,0:T(4,128)S(1)} %get-tuple-element.40.after), channel_id=1, replica_groups=mesh['gx'=8,'gy'=32] {'gx'}, dimensions={0} | all-to-all | bytes 4096 | tf_op jit(solution)/shard_map/all_to_all | solution.py:560
  25.4 0.9 %shard_map.157.refs_7_.after = f32[32,4,128]{2,1,0:T(4,128)} custom-call(f32[8,4,16]{2,1,0:T(4,128)S(1)} %all_to_all.10.rows, f32[128,128]{1,0:T(8,128)S(1)} %get-tuple-element.43.modes_xz), custom_call_target="tpu_custom_call" | custom-call | tf_op jit(solution)/shard_map/pallas_call | solution.py:578
  26.2 0.0 copy-done.5
  26.2 0.0 copy-done.9
  26.2 0.0 copy-done.10
  26.3 0.6 shard_map.158
  26.9 0.0 collective-permute-done.2.ylo
  26.9 0.0 collective-permute-done.3.yhi
  26.9 8.5 %shard_map.159 = (bf16[5120,256]{1,0:T(8,128)(2,1)S(1)}, bf16[160,256]{1,0:T(8,128)(2,1)S(1)}, bf16[160,256]{1,0:T(8,128)(2,1)}, bf16[512,256]{1,0:T(8,128)(2,1)S(1)}, bf16[512,256]{1,0:T(8,128)(2,1)}) custom-call(f32[4096,256]{1,0:T(8,128)} %bitcast.20, bf16[128,256]{1,0:T(8,128)(2,1)S(1)} %collective-permute-done.xlo, ...), custom_call_target="tpu_custom_call" | custom-call | tf_op jit(solution)/shard_map/pallas_call | solution.py:368
  35.3 0.0 copy-start.11
  35.4 0.1 collective-permute-start.6
  35.4 5.3 %collective-permute-start.7 = (bf16[512,256]{1,0:T(8,128)(2,1)S(1)}, bf16[512,256]{1,0:T(8,128)(2,1)}, u32[]{:S(2)}, u32[]{:S(2)}) collective-permute-start(bf16[512,256]{1,0:T(8,128)(2,1)S(1)} %get-tuple-element.54.refs_6_), channel_id=1, source_target_pairs={{0,31},{1,0},{2,1},{3,2},{4,3},{5,4},{6,5},{7,6},{8,7},{9,8},{10,9... | collective-permute-start | bytes 786440 | tf_op jit(solution)/shard_map/ppermute | solution.py:556
  40.8 5.5 %all-to-all-start.1 = ((f32[32,4,128]{2,1,0:T(4,128)}), f32[32,4,128]{2,1,0:T(4,128)S(1)}, u32[]{:S(2)}, u32[]{:S(2)}) async-start(f32[32,4,128]{2,1,0:T(4,128)} %shard_map.157.refs_7_.after), calls=%async_computation.1 | async-start | bytes 131072 | tf_op jit(solution)/shard_map/all_to_all | solution.py:560
  46.3 0.0 collective-permute-start.4
  46.4 1.7 %collective-permute-start.5 = (bf16[160,256]{1,0:T(8,128)(2,1)}, bf16[160,256]{1,0:T(8,128)(2,1)S(1)}, u32[]{:S(2)}, u32[]{:S(2)}) collective-permute-start(bf16[160,256]{1,0:T(8,128)(2,1)} %copy-done.11), channel_id=1, source_target_pairs={{0,224},{32,0},{64,32},{96,64},{128,96},{160,128},{192,160},{224,1... | collective-permute-start | bytes 245768 | tf_op jit(solution)/shard_map/ppermute | solution.py:556
  48.1 8.2 %all-to-all-done.1.rows = f32[32,4,128]{2,1,0:T(4,128)S(1)} async-done(((f32[32,4,128]{2,1,0:T(4,128)}), f32[32,4,128]{2,1,0:T(4,128)S(1)}, u32[]{:S(2)}, u32[]{:S(2)}) %all-to-all-start.1) | async-done | bytes 65568 | tf_op jit(solution)/shard_map/all_to_all | solution.py:560
  56.3 2.4 %shard_map.160.after.shape = bf16[1024,256]{1,0:T(8,128)(2,1)S(1)} custom-call(f32[32,4,128]{2,1,0:T(4,128)S(1)} %all-to-all-done.1.rows, f32[128,128]{1,0:T(8,128)S(1)} %get-tuple-element.43.modes_xz, f32[128,128]{1,0:T(8,128)} %refs_0_.3, f32[1,32]{1,0:T(1,128)} %bitcast.21, f32[1,128]{1,0:T(1,128)} %bitcast.22, f32[1,4]{1,0:T(1,128)} %bitcast.23, ...), custom_call_target="tpu_custom_call" | custom-call | tf_op jit(solution)/shard_map/pallas_call | solution.py:599
  58.7 0.0 collective-permute-done.4.rxlo
  58.7 0.0 collective-permute-done.5.rxhi
  58.7 1.5 %collective-permute-start.9 = (bf16[32,256]{1,0:T(8,128)(2,1)S(1)}, bf16[32,256]{1,0:T(8,128)(2,1)S(1)}, u32[]{:S(2)}, u32[]{:S(2)}) collective-permute-start(bf16[32,256]{1,0:T(8,128)(2,1)S(1)} %get-tuple-element.62), channel_id=1, source_target_pairs={{0,31},{1,0},{2,1},{3,2},{4,3},{5,4},{6,5},{7,6},{8,7},{9,8},{10,9... | collective-permute-start | bytes 49160 | tf_op jit(solution)/shard_map/ppermute | solution.py:556
  60.2 0.6 collective-permute-start.8
  60.8 2.1 %shard_map.162 = (f32[128,32,256]{2,1,0:T(8,128)}, f32[128,16,256]{2,1,0:T(8,128)S(1)}) custom-call(bf16[5120,256]{1,0:T(8,128)(2,1)S(1)} %get-tuple-element.52.field, bf16[128,192]{1,0:T(8,128)(2,1)S(1)} %get-tuple-element.53.wfin, bf16[1024,256]{1,0:T(8,128)(2,1)S(1)} %shard_map.160.after.shape, bf16[160,256]{1,0:T(8,128)(2,1)S(1)} %collective-permute-done.4.rxlo, ...), custom_call_target="tpu_custom_call" | custom-call | tf_op jit(solution)/shard_map/pallas_call | solution.py:497
  62.9 0.0 collective-permute-done.9.cornhi
  62.9 4.4 %collective-permute-done.8.cornlo = bf16[32,256]{1,0:T(8,128)(2,1)S(1)} collective-permute-done((bf16[32,256]{1,0:T(8,128)(2,1)S(1)}, bf16[32,256]{1,0:T(8,128)(2,1)S(1)}, u32[]{:S(2)}, u32[]{:S(2)}) %collective-permute-start.8) | collective-permute-done | bytes 16416 | tf_op jit(solution)/shard_map/ppermute | solution.py:556
  67.3 0.0 collective-permute-done.6.rylo
  67.3 0.0 collective-permute-done.7.ryhi
  67.3 2.6 %combine.1 = f32[128,32,256]{2,1,0:T(8,128)} custom-call(f32[128,32,256]{2,1,0:T(8,128)} %get-tuple-element.58.partial, f32[128,16,256]{2,1,0:T(8,128)S(1)} %get-tuple-element.59.rims, bf16[64,32]{1,0:T(8,128)(2,1)S(1)} %get-tuple-element.60.spread, bf16[512,256]{1,0:T(8,128)(2,1)S(1)} %collective-permute-done.6.rylo, ...), custom_call_target="tpu_custom_call", output_to_operand_aliasing={{}: (0, {})} | custom-call | tf_op jit(solution)/shard_map/combine/pallas_call | solution.py:542
  (9 shorter events, 0.0 us)
Async XLA Ops:
  0.0 26.2 %copy-start.5 = (bf16[32,4]{0,1:T(4,128)(2,1)S(1)}, bf16[32,4]{0,1:T(4,128)(2,1)}, u32[]{:S(2)}) copy-start(bf16[32,4]{0,1:T(4,128)(2,1)} %param.24) | copy-start | bytes 772
  0.0 5.5 %copy-start.7 = (f32[4,4]{1,0:T(4,128)S(1)}, f32[4,4]{1,0:T(4,128)}, u32[]{:S(2)}) copy-start(f32[4,4]{1,0:T(4,128)} %mode_z.1) | copy-start | bytes 196
  0.0 5.5 %copy-start.2 = (f32[32,32]{1,0:T(8,128)S(1)}, f32[32,32]{1,0:T(8,128)}, u32[]{:S(2)}) copy-start(f32[32,32]{1,0:T(8,128)} %mode_x.1) | copy-start | bytes 12292
  0.0 5.5 %copy-start.4 = (bf16[256,4]{0,1:T(4,128)(2,1)S(1)}, bf16[256,4]{0,1:T(4,128)(2,1)}, u32[]{:S(2)}) copy-start(bf16[256,4]{0,1:T(4,128)(2,1)} %param.25) | copy-start | bytes 6148
  0.0 5.5 %copy-start.6 = (bf16[128,4]{0,1:T(4,128)(2,1)S(1)}, bf16[128,4]{0,1:T(4,128)(2,1)}, u32[]{:S(2)}) copy-start(bf16[128,4]{0,1:T(4,128)(2,1)} %param.23) | copy-start | bytes 3076
  0.0 26.2 %copy-start.9 = (f32[256]{0:T(256)S(1)}, f32[256]{0:T(256)}, u32[]{:S(2)}) copy-start(f32[256]{0:T(256)} %param.22) | copy-start | bytes 3076
  0.0 26.2 %copy-start.10 = (f32[40]{0:T(128)S(1)}, f32[40]{0:T(128)}, u32[]{:S(2)}) copy-start(f32[40]{0:T(128)} %param.21) | copy-start | bytes 484
  0.1 26.2 %copy-start.8 = (f32[136]{0:T(256)S(1)}, f32[136]{0:T(256)}, u32[]{:S(2)}) copy-start(f32[136]{0:T(256)} %param.20) | copy-start | bytes 1636
  0.1 26.2 %copy-start = (bf16[256,256]{1,0:T(8,128)(2,1)S(1)}, bf16[256,256]{1,0:T(8,128)(2,1)}, u32[]{:S(2)}) copy-start(bf16[256,256]{1,0:T(8,128)(2,1)} %refs_2_.1) | copy-start | bytes 393220
  0.1 26.2 %copy-start.3 = (bf16[40,40]{1,0:T(8,128)(2,1)S(1)}, bf16[40,40]{1,0:T(8,128)(2,1)}, u32[]{:S(2)}) copy-start(bf16[40,40]{1,0:T(8,128)(2,1)} %refs_1_.1) | copy-start | bytes 9604
  0.1 26.2 %copy-start.1 = (bf16[136,136]{1,0:T(8,128)(2,1)S(1)}, bf16[136,136]{1,0:T(8,128)(2,1)}, u32[]{:S(2)}) copy-start(bf16[136,136]{1,0:T(8,128)(2,1)} %refs_0_.2) | copy-start | bytes 110980
  3.7 3.7 %collective-permute-start = (bf16[128,256]{1,0:T(8,128)(2,1)S(1)}, bf16[128,256]{1,0:T(8,128)(2,1)S(1)}, u32[]{:S(2)}, u32[]{:S(2)}) collective-permute-start(bf16[128,256]{1,0:T(8,128)(2,1)S(1)} %get-tuple-element.34), channel_id=1, source_target_pairs={{0,32},{32,64},{64,96},{96,128},{128,160},{160,192},{192,224},{224... | collective-permute-start | bytes 196616 | tf_op jit(solution)/shard_map/ppermute | solution.py:556
  3.8 3.7 %collective-permute-start.1 = (bf16[128,256]{1,0:T(8,128)(2,1)S(1)}, bf16[128,256]{1,0:T(8,128)(2,1)S(1)}, u32[]{:S(2)}, u32[]{:S(2)}) collective-permute-start(bf16[128,256]{1,0:T(8,128)(2,1)S(1)} %get-tuple-element.35), channel_id=1, source_target_pairs={{0,224},{32,0},{64,32},{96,64},{128,96},{160,128},{192,160},{224,1... | collective-permute-start | bytes 196616 | tf_op jit(solution)/shard_map/ppermute | solution.py:556
  7.6 19.3 %collective-permute-start.2 = (bf16[544,256]{1,0:T(8,128)(2,1)S(1)}, bf16[544,256]{1,0:T(8,128)(2,1)S(1)}, u32[]{:S(2)}, u32[]{:S(2)}) collective-permute-start(bf16[544,256]{1,0:T(8,128)(2,1)S(1)} %get-tuple-element.41), channel_id=1, source_target_pairs={{0,1},{1,2},{2,3},{3,4},{4,5},{5,6},{6,7},{7,8},{8,9},{9,10},{10,1... | collective-permute-start | bytes 835592 | tf_op jit(solution)/shard_map/ppermute | solution.py:556
  9.2 17.7 %collective-permute-start.3 = (bf16[544,256]{1,0:T(8,128)(2,1)S(1)}, bf16[544,256]{1,0:T(8,128)(2,1)S(1)}, u32[]{:S(2)}, u32[]{:S(2)}) collective-permute-start(bf16[544,256]{1,0:T(8,128)(2,1)S(1)} %get-tuple-element.42), channel_id=1, source_target_pairs={{0,31},{1,0},{2,1},{3,2},{4,3},{5,4},{6,5},{7,6},{8,7},{9,8},{10,9... | collective-permute-start | bytes 835592 | tf_op jit(solution)/shard_map/ppermute | solution.py:556
  35.3 11.0 %copy-start.11 = (bf16[160,256]{1,0:T(8,128)(2,1)}, bf16[160,256]{1,0:T(8,128)(2,1)S(1)}, u32[]{:S(2)}) copy-start(bf16[160,256]{1,0:T(8,128)(2,1)S(1)} %get-tuple-element.56) | copy-start | bytes 245764
  35.4 31.9 %collective-permute-start.6 = (bf16[512,256]{1,0:T(8,128)(2,1)}, bf16[512,256]{1,0:T(8,128)(2,1)S(1)}, u32[]{:S(2)}, u32[]{:S(2)}) collective-permute-start(bf16[512,256]{1,0:T(8,128)(2,1)} %get-tuple-element.61), channel_id=1, source_target_pairs={{0,1},{1,2},{2,3},{3,4},{4,5},{5,6},{6,7},{7,8},{8,9},{9,10},{10,1... | collective-permute-start | bytes 786440 | tf_op jit(solution)/shard_map/ppermute | solution.py:556
  35.4 31.8 %collective-permute-start.7 = (bf16[512,256]{1,0:T(8,128)(2,1)S(1)}, bf16[512,256]{1,0:T(8,128)(2,1)}, u32[]{:S(2)}, u32[]{:S(2)}) collective-permute-start(bf16[512,256]{1,0:T(8,128)(2,1)S(1)} %get-tuple-element.54.refs_6_), channel_id=1, source_target_pairs={{0,31},{1,0},{2,1},{3,2},{4,3},{5,4},{6,5},{7,6},{8,7},{9,8},{10,9... | collective-permute-start | bytes 786440 | tf_op jit(solution)/shard_map/ppermute | solution.py:556
  40.8 15.5 %all-to-all-start.1 = ((f32[32,4,128]{2,1,0:T(4,128)}), f32[32,4,128]{2,1,0:T(4,128)S(1)}, u32[]{:S(2)}, u32[]{:S(2)}) async-start(f32[32,4,128]{2,1,0:T(4,128)} %shard_map.157.refs_7_.after), calls=%async_computation.1 | async-start | bytes 131072 | tf_op jit(solution)/shard_map/all_to_all | solution.py:560
  46.3 12.4 %collective-permute-start.4 = (bf16[160,256]{1,0:T(8,128)(2,1)}, bf16[160,256]{1,0:T(8,128)(2,1)S(1)}, u32[]{:S(2)}, u32[]{:S(2)}) collective-permute-start(bf16[160,256]{1,0:T(8,128)(2,1)} %get-tuple-element.55), channel_id=1, source_target_pairs={{0,32},{32,64},{64,96},{96,128},{128,160},{160,192},{192,224},{224... | collective-permute-start | bytes 245768 | tf_op jit(solution)/shard_map/ppermute | solution.py:556
  46.4 12.3 %collective-permute-start.5 = (bf16[160,256]{1,0:T(8,128)(2,1)}, bf16[160,256]{1,0:T(8,128)(2,1)S(1)}, u32[]{:S(2)}, u32[]{:S(2)}) collective-permute-start(bf16[160,256]{1,0:T(8,128)(2,1)} %copy-done.11), channel_id=1, source_target_pairs={{0,224},{32,0},{64,32},{96,64},{128,96},{160,128},{192,160},{224,1... | collective-permute-start | bytes 245768 | tf_op jit(solution)/shard_map/ppermute | solution.py:556
  58.7 4.2 %collective-permute-start.9 = (bf16[32,256]{1,0:T(8,128)(2,1)S(1)}, bf16[32,256]{1,0:T(8,128)(2,1)S(1)}, u32[]{:S(2)}, u32[]{:S(2)}) collective-permute-start(bf16[32,256]{1,0:T(8,128)(2,1)S(1)} %get-tuple-element.62), channel_id=1, source_target_pairs={{0,31},{1,0},{2,1},{3,2},{4,3},{5,4},{6,5},{7,6},{8,7},{9,8},{10,9... | collective-permute-start | bytes 49160 | tf_op jit(solution)/shard_map/ppermute | solution.py:556
  60.2 7.1 %collective-permute-start.8 = (bf16[32,256]{1,0:T(8,128)(2,1)S(1)}, bf16[32,256]{1,0:T(8,128)(2,1)S(1)}, u32[]{:S(2)}, u32[]{:S(2)}) collective-permute-start(bf16[32,256]{1,0:T(8,128)(2,1)S(1)} %get-tuple-element.57.after), channel_id=1, source_target_pairs={{0,1},{1,2},{2,3},{3,4},{4,5},{5,6},{6,7},{7,8},{8,9},{9,10},{10,1... | collective-permute-start | bytes 49160 | tf_op jit(solution)/shard_map/ppermute | solution.py:556

commit v3 on v2

--- a/solution.py
+++ b/solution.py
@@ -96,10 +96,8 @@
 
 def selection(cyt):
     row, col = iotas((3 * RIM, OWN))
-    y, k = iotas((CY, OWN))
-    spread = dot(cyt, pick((k & 31) == y)).astype(bf16)
-    row4, n = iotas((3 * RIM, MODES))
-    modes = dot(pick((row4 & 3) == n), spread)
+    modes = jnp.concatenate([cyt.astype(f32)] * GX, 1)
+    modes = jnp.concatenate([jnp.concatenate([modes] * 2, 0)] * (3 * RIM // 8), 0)
     plane = ((row >> 2) & 3) == (col >> 5)
     inner = col & 31
     target = jnp.where(row < RIM, row & 3, CY - OV + (row & 3))
@@ -274,7 +272,8 @@
 
 def solve_kernel(
     residual, xlo, xhi, ylo, yhi, wy, wyt, wx, wxt, lz, lzt, exb, eyz, after,
-    kept, out_xlo, out_xhi, out_ylo, out_yhi, field, mid, spec, buf, sems,
+    kept, far_xlo, far_xhi, far_ylo, far_yhi, field, mid, spec, buf, sems,
+    out_xlo, out_xhi, out_ylo, out_yhi, sems_out,
 ):
     def put(rows, value):
         field[0, rows, :] = value[:, :128]
@@ -359,7 +358,23 @@
         out_yhi[at, :] = out[RIM:]
         return carry
 
-    lax.fori_loop(0, BLOCKS, last, 0, unroll=16)
+    copies = [
+        pltpu.make_async_copy(out_xlo, far_xlo, sems_out.at[0]),
+        pltpu.make_async_copy(out_xhi, far_xhi, sems_out.at[1]),
+    ]
+    for copy in copies:
+        copy.start()
+    half = BLOCKS // 2
+    for i in range(2):
+        lax.fori_loop(i * half, (i + 1) * half, last, 0, unroll=half)
+        at = pl.ds(i * half * RIM, half * RIM)
+        for j, (near, far) in enumerate(((out_ylo, far_ylo), (out_yhi, far_yhi))):
+            sem = sems_out.at[2 + 2 * i + j]
+            copy = pltpu.make_async_copy(near.at[at, :], far.at[at, :], sem)
+            copy.start()
+            copies.append(copy)
+    for copy in copies:
+        copy.wait()
 
 
 def solve(*args):
@@ -370,10 +385,13 @@
         (sds((BLOCKS * ROWS, NZ), bf16), strip, strip, rim, rim),
         [HBM] + [VM] * 12 + [ANY],
         WIDE_SOLVE,
+        out_specs=(VM, ANY, ANY, ANY, ANY),
         scratch=[
             pltpu.VMEM((2, EX * EY, NZ // 2), f32), pltpu.VMEM((EX * EY, NZ), f32),
             pltpu.VMEM((EX * EY, NZ), bf16), pltpu.VMEM((CELLS, NZ), f32),
-            pltpu.SemaphoreType.DMA((CHUNKS,)),
+            pltpu.SemaphoreType.DMA((CHUNKS,)), pltpu.VMEM((ROWS, NZ), bf16),
+            pltpu.VMEM((ROWS, NZ), bf16), pltpu.VMEM((CX * OV, NZ), bf16),
+            pltpu.VMEM((CX * OV, NZ), bf16), pltpu.SemaphoreType.DMA((6,)),
         ],
     )(*args)
 
@@ -389,7 +407,7 @@
     return call(turn_kernel, (both, both), [VM] * 2 + [ANY], 4)(*args)
 
 
-def restrict_kernel(along_y, cxt, czt, mode_x, mode_z, out, modes_xz):
+def restrict_kernel(along_y, cxt, czt, out):
     bx = basis_x(cxt[...])
     high, low = split(along_y[...])
     both = dot(bx, high) + dot(bx, low)
@@ -397,6 +415,9 @@
     flat = jnp.concatenate([own[m * MODES : (m + 1) * MODES] for m in range(MODES)], 1)
     for i in range(out.shape[0]):
         out[i] = flat
+
+
+def modes_kernel(mode_x, mode_z, after, modes_xz):
     to_a, _ = modes_a()
     r, i = iotas((128, 32))
     part_x = expand(expand(mode_x[...], rows=pick((r >> 2) == i)), cols=to_a)
@@ -568,13 +589,14 @@
     first_x, last_x, rim_lo, rim_hi, along_y, sel = load(cells, coarse_y)
     xlo = shift(last_x, "gx", 1)
     xhi = shift(first_x, "gx", -1)
-    own_coarse, modes_xz = call(
-        restrict_kernel, (sds((8, MODES, 16), f32), sds((128, 128), f32)), [VM] * 5, 8
-    )(along_y, coarse_x.T, coarse_z.T, mode_x, mode_z)
+    own_coarse = call(restrict_kernel, sds((8, MODES, 16), f32), [VM] * 3, 8)(
+        along_y, coarse_x.T, coarse_z.T
+    )
     rows = exchange(own_coarse, "gx")
     down, up = corners(sel, rim_lo, rim_hi, xlo, xhi, own_coarse)
     ylo = shift(up, "gy", 1)
     yhi = shift(down, "gy", -1)
+    modes_xz = call(modes_kernel, sds((128, 128), f32), [VM, VM, ANY], 4)(mode_x, mode_z, up)
     part = call(coarse_x_kernel, sds((32, MODES, 128), f32), [VM] * 2, 4)(rows, modes_xz)
     rows = exchange(part, "gy")
 

time: 70.1 us -> 69.6 us (level)
  the two profiles are of different devices: /device:TPU:2 before, /device:TPU:4 now
where the time goes in v3:
time: 69.6 us; the launch traced here: 69.3 us
  starting transfers between devices  28.2 us (41%)
  Pallas kernels  21.4 us (31%)
  waiting for transfers between devices  18.2 us (26%)
  local copies, waits for them, and re-layouts  1.3 us (2%)
    ppermute x10, starting transfers between devices, shift(): return lax.ppermute(x, axis, [(i, (i + step) % size) for i in range(size)])  18.7 us
    all_to_all x2, waiting for transfers between devices, exchange(): return lax.all_to_all(x, axis, 0, 0)  10.8 us
    all_to_all x2, starting transfers between devices, exchange(): return lax.all_to_all(x, axis, 0, 0)  9.5 us
    pallas_call x1, Pallas kernels, solve(): call(solve_kernel, (sds((BLOCKS * ROWS, NZ), bf16), strip, strip, rim, ri...  8.59 us
    ppermute x10, waiting for transfers between devices, shift(): return lax.ppermute(x, axis, [(i, (i + step) % size) for i in range(size)])  7.4 us
    pallas_call x1, Pallas kernels, load(): call(load_kernel, (sds((OWN, NZ), bf16), sds((OWN, NZ), bf16), rim, rim,...  3.49 us
    pallas_call x1, Pallas kernels, local(): call(coarse_kernel, sds((2 * CX * MODES, NZ), bf16), [VM] * 2 + [HBM] * l...  2.36 us
    pallas_call x1, Pallas kernels, finish(): call(finish_kernel, (sds((CX, CY, NZ), f32), sds((CX, 16, NZ), f32)), [VM...  2.09 us
  transfers between devices with their start and end apart: 12, of which 5 were waited for; matrix products, arithmetic and copies ran while one was open for 0% of the time, Pallas kernels for 11%

profile of v3, /device:TPU:4, one launch (start us, length us, event | category | flops | bytes accessed | tf_op | source)
XLA Modules:
  0.0 69.3 jit_solution(17293023548079062475)
XLA Ops:
  0.0 0.0 copy-start.7
  0.0 0.0 copy-start.2
  0.0 0.0 copy-start.9
  0.0 0.0 copy-start.10
  0.0 0.0 copy-start.8
  0.1 0.0 copy-start
  0.1 0.0 copy-start.3
  0.1 0.0 copy-start.1
  0.1 3.5 %shard_map.154 = (bf16[128,256]{1,0:T(8,128)(2,1)S(1)}, bf16[128,256]{1,0:T(8,128)(2,1)S(1)}, bf16[512,256]{1,0:T(8,128)(2,1)S(1)}, bf16[512,256]{1,0:T(8,128)(2...) custom-call(f32[4096,256]{1,0:T(8,128)} %bitcast.19, bf16[4,32]{1,0:T(4,128)(2,1)} %bitcast.12), custom_call_target="tpu_custom_call" | custom-call | tf_op jit(solution)/shard_map/pallas_call | solution.py:143
  3.6 0.0 collective-permute-start
  3.6 1.7 %collective-permute-start.1 = (bf16[128,256]{1,0:T(8,128)(2,1)S(1)}, bf16[128,256]{1,0:T(8,128)(2,1)S(1)}, u32[]{:S(2)}, u32[]{:S(2)}) collective-permute-start(bf16[128,256]{1,0:T(8,128)(2,1)S(1)} %get-tuple-element.33), channel_id=1, source_target_pairs={{0,224},{32,0},{64,32},{96,64},{128,96},{160,128},{192,160},{224,1... | collective-permute-start | bytes 196616 | tf_op jit(solution)/shard_map/ppermute | solution.py:577
  5.3 0.0 copy-done.4
  5.3 1.3 %shard_map.155.after = f32[8,4,16]{2,1,0:T(4,128)} custom-call(f32[512,256]{1,0:T(8,128)S(1)} %get-tuple-element.37.along_y, bf16[4,128]{1,0:T(4,128)(2,1)S(1)} %bitcast.15, bf16[4,256]{1,0:T(4,128)(2,1)S(1)} %bitcast.11), custom_call_target="tpu_custom_call" | custom-call | tf_op jit(solution)/shard_map/pallas_call | solution.py:592
  6.6 0.6 collective-permute-done.xlo
  7.3 0.0 collective-permute-done.1.xhi
  7.3 0.1 shard_map.156
  7.4 8.3 %collective-permute-start.3 = (bf16[544,256]{1,0:T(8,128)(2,1)S(1)}, bf16[544,256]{1,0:T(8,128)(2,1)S(1)}, u32[]{:S(2)}, u32[]{:S(2)}) collective-permute-start(bf16[544,256]{1,0:T(8,128)(2,1)S(1)} %get-tuple-element.39), channel_id=1, source_target_pairs={{0,31},{1,0},{2,1},{3,2},{4,3},{5,4},{6,5},{7,6},{8,7},{9,8},{10,9... | collective-permute-start | bytes 835592 | tf_op jit(solution)/shard_map/ppermute | solution.py:577
  15.8 0.0 collective-permute-start.2
  15.8 5.7 %all-to-all-start = ((f32[8,4,16]{2,1,0:T(4,128)}), f32[8,4,16]{2,1,0:T(4,128)S(1)}, u32[]{:S(2)}, u32[]{:S(2)}) async-start(f32[8,4,16]{2,1,0:T(4,128)} %shard_map.155.after), calls=%async_computation | async-start | bytes 32768 | tf_op jit(solution)/shard_map/all_to_all | solution.py:581
  21.4 0.0 copy-done.7
  21.4 0.4 shard_map.157.modes_xz
  21.9 2.5 %all-to-all-done.rows = f32[8,4,16]{2,1,0:T(4,128)S(1)} async-done(((f32[8,4,16]{2,1,0:T(4,128)}), f32[8,4,16]{2,1,0:T(4,128)S(1)}, u32[]{:S(2)}, u32[]{:S(2)}) %all-to-all-start) | async-done | bytes 2080 | tf_op jit(solution)/shard_map/all_to_all | solution.py:581
  24.4 0.9 %shard_map.158.refs_7_.after = f32[32,4,128]{2,1,0:T(4,128)} custom-call(f32[8,4,16]{2,1,0:T(4,128)S(1)} %all-to-all-done.rows, f32[128,128]{1,0:T(8,128)S(1)} %shard_map.157.modes_xz), custom_call_target="tpu_custom_call" | custom-call | tf_op jit(solution)/shard_map/pallas_call | solution.py:600
  25.3 0.0 copy-done.10
  25.3 0.6 shard_map.159
  25.9 0.0 collective-permute-done.3.yhi
  25.9 2.7 %collective-permute-done.2.ylo = bf16[544,256]{1,0:T(8,128)(2,1)S(1)} collective-permute-done((bf16[544,256]{1,0:T(8,128)(2,1)S(1)}, bf16[544,256]{1,0:T(8,128)(2,1)S(1)}, u32[]{:S(2)}, u32[]{:S(2)}) %collective-permute-start.2) | collective-permute-done | bytes 278560 | tf_op jit(solution)/shard_map/ppermute | solution.py:577
  28.6 8.6 %shard_map.160 = (bf16[5120,256]{1,0:T(8,128)(2,1)S(1)}, bf16[160,256]{1,0:T(8,128)(2,1)S(1)}, bf16[160,256]{1,0:T(8,128)(2,1)S(1)}, bf16[512,256]{1,0:T(8,128)(2,1)}, bf16[512,256]{1,0:T(8,128)(2,1)}) custom-call(f32[4096,256]{1,0:T(8,128)} %bitcast.20, bf16[128,256]{1,0:T(8,128)(2,1)S(1)} %collective-permute-done.xlo, ...), custom_call_target="tpu_custom_call" | custom-call | tf_op jit(solution)/shard_map/pallas_call | solution.py:383
  37.2 0.0 copy-start.12
  37.2 0.6 copy-done.12
  37.8 0.0 collective-permute-start.6
  37.8 0.6 copy-done.11
  38.4 4.7 %collective-permute-start.7 = (bf16[512,256]{1,0:T(8,128)(2,1)}, bf16[512,256]{1,0:T(8,128)(2,1)S(1)}, u32[]{:S(2)}, u32[]{:S(2)}) collective-permute-start(bf16[512,256]{1,0:T(8,128)(2,1)} %get-tuple-element.50.refs_6_), channel_id=1, source_target_pairs={{0,31},{1,0},{2,1},{3,2},{4,3},{5,4},{6,5},{7,6},{8,7},{9,8},{10,9... | collective-permute-start | bytes 786440 | tf_op jit(solution)/shard_map/ppermute | solution.py:577
  43.1 3.8 %all-to-all-start.1 = ((f32[32,4,128]{2,1,0:T(4,128)}), f32[32,4,128]{2,1,0:T(4,128)S(1)}, u32[]{:S(2)}, u32[]{:S(2)}) async-start(f32[32,4,128]{2,1,0:T(4,128)} %shard_map.158.refs_7_.after), calls=%async_computation.1 | async-start | bytes 131072 | tf_op jit(solution)/shard_map/all_to_all | solution.py:581
  47.0 0.0 collective-permute-start.4
  47.0 1.7 %collective-permute-start.5 = (bf16[160,256]{1,0:T(8,128)(2,1)}, bf16[160,256]{1,0:T(8,128)(2,1)S(1)}, u32[]{:S(2)}, u32[]{:S(2)}) collective-permute-start(bf16[160,256]{1,0:T(8,128)(2,1)} %copy-done.11), channel_id=1, source_target_pairs={{0,224},{32,0},{64,32},{96,64},{128,96},{160,128},{192,160},{224,1... | collective-permute-start | bytes 245768 | tf_op jit(solution)/shard_map/ppermute | solution.py:577
  48.8 8.3 %all-to-all-done.1.rows = f32[32,4,128]{2,1,0:T(4,128)S(1)} async-done(((f32[32,4,128]{2,1,0:T(4,128)}), f32[32,4,128]{2,1,0:T(4,128)S(1)}, u32[]{:S(2)}, u32[]{:S(2)}) %all-to-all-start.1) | async-done | bytes 65568 | tf_op jit(solution)/shard_map/all_to_all | solution.py:581
  57.0 2.4 %shard_map.161.after.shape = bf16[1024,256]{1,0:T(8,128)(2,1)S(1)} custom-call(f32[32,4,128]{2,1,0:T(4,128)S(1)} %all-to-all-done.1.rows, f32[128,128]{1,0:T(8,128)S(1)} %shard_map.157.modes_xz, f32[128,128]{1,0:T(8,128)} %refs_0_.3, f32[1,32]{1,0:T(1,128)} %bitcast.21, f32[1,128]{1,0:T(1,128)} %bitcast.22, f32[1,4]{1,0:T(1,128)} %bitcast.23, ...), custom_call_target="tpu_custom_call" | custom-call | tf_op jit(solution)/shard_map/pallas_call | solution.py:621
  59.4 0.0 collective-permute-done.4.rxlo
  59.4 0.0 collective-permute-done.5.rxhi
  59.4 1.2 %collective-permute-start.9 = (bf16[32,256]{1,0:T(8,128)(2,1)S(1)}, bf16[32,256]{1,0:T(8,128)(2,1)S(1)}, u32[]{:S(2)}, u32[]{:S(2)}) collective-permute-start(bf16[32,256]{1,0:T(8,128)(2,1)S(1)} %get-tuple-element.58), channel_id=1, source_target_pairs={{0,31},{1,0},{2,1},{3,2},{4,3},{5,4},{6,5},{7,6},{8,7},{9,8},{10,9... | collective-permute-start | bytes 49160 | tf_op jit(solution)/shard_map/ppermute | solution.py:577
  60.6 0.9 %collective-permute-start.8 = (bf16[32,256]{1,0:T(8,128)(2,1)S(1)}, bf16[32,256]{1,0:T(8,128)(2,1)S(1)}, u32[]{:S(2)}, u32[]{:S(2)}) collective-permute-start(bf16[32,256]{1,0:T(8,128)(2,1)S(1)} %get-tuple-element.53.after), channel_id=1, source_target_pairs={{0,1},{1,2},{2,3},{3,4},{4,5},{5,6},{6,7},{7,8},{8,9},{9,10},{10,1... | collective-permute-start | bytes 49160 | tf_op jit(solution)/shard_map/ppermute | solution.py:577
  61.5 2.1 %shard_map.163 = (f32[128,32,256]{2,1,0:T(8,128)}, f32[128,16,256]{2,1,0:T(8,128)S(1)}) custom-call(bf16[5120,256]{1,0:T(8,128)(2,1)S(1)} %get-tuple-element.48.field, bf16[128,192]{1,0:T(8,128)(2,1)S(1)} %get-tuple-element.49.wfin, bf16[1024,256]{1,0:T(8,128)(2,1)S(1)} %shard_map.161.after.shape, bf16[160,256]{1,0:T(8,128)(2,1)S(1)} %collective-permute-done.4.rxlo, ...), custom_call_target="tpu_custom_call" | custom-call | tf_op jit(solution)/shard_map/pallas_call | solution.py:518
  63.6 0.0 collective-permute-done.9.cornhi
  63.6 4.1 %collective-permute-done.8.cornlo = bf16[32,256]{1,0:T(8,128)(2,1)S(1)} collective-permute-done((bf16[32,256]{1,0:T(8,128)(2,1)S(1)}, bf16[32,256]{1,0:T(8,128)(2,1)S(1)}, u32[]{:S(2)}, u32[]{:S(2)}) %collective-permute-start.8) | collective-permute-done | bytes 16416 | tf_op jit(solution)/shard_map/ppermute | solution.py:577
  67.7 0.0 collective-permute-done.6.rylo
  67.7 0.0 collective-permute-done.7.ryhi
  67.7 1.6 %combine.1 = f32[128,32,256]{2,1,0:T(8,128)} custom-call(f32[128,32,256]{2,1,0:T(8,128)} %get-tuple-element.54.partial, f32[128,16,256]{2,1,0:T(8,128)S(1)} %get-tuple-element.55.rims, bf16[64,32]{1,0:T(8,128)(2,1)S(1)} %get-tuple-element.56.spread, bf16[512,256]{1,0:T(8,128)(2,1)S(1)} %collective-permute-done.6.rylo, ...), custom_call_target="tpu_custom_call", output_to_operand_aliasing={{}: (0, {})} | custom-call | tf_op jit(solution)/shard_map/combine/pallas_call | solution.py:563
  (13 shorter events, 0.0 us)
Async XLA Ops:
  0.0 25.3 %copy-start.5 = (bf16[32,4]{0,1:T(4,128)(2,1)S(1)}, bf16[32,4]{0,1:T(4,128)(2,1)}, u32[]{:S(2)}) copy-start(bf16[32,4]{0,1:T(4,128)(2,1)} %param.24) | copy-start | bytes 772
  0.0 5.3 %copy-start.4 = (bf16[256,4]{0,1:T(4,128)(2,1)S(1)}, bf16[256,4]{0,1:T(4,128)(2,1)}, u32[]{:S(2)}) copy-start(bf16[256,4]{0,1:T(4,128)(2,1)} %param.25) | copy-start | bytes 6148
  0.0 5.3 %copy-start.6 = (bf16[128,4]{0,1:T(4,128)(2,1)S(1)}, bf16[128,4]{0,1:T(4,128)(2,1)}, u32[]{:S(2)}) copy-start(bf16[128,4]{0,1:T(4,128)(2,1)} %param.23) | copy-start | bytes 3076
  0.0 21.4 %copy-start.7 = (f32[4,4]{1,0:T(4,128)S(1)}, f32[4,4]{1,0:T(4,128)}, u32[]{:S(2)}) copy-start(f32[4,4]{1,0:T(4,128)} %mode_z.1) | copy-start | bytes 196
  0.0 21.4 %copy-start.2 = (f32[32,32]{1,0:T(8,128)S(1)}, f32[32,32]{1,0:T(8,128)}, u32[]{:S(2)}) copy-start(f32[32,32]{1,0:T(8,128)} %mode_x.1) | copy-start | bytes 12292
  0.0 25.2 %copy-start.9 = (f32[256]{0:T(256)S(1)}, f32[256]{0:T(256)}, u32[]{:S(2)}) copy-start(f32[256]{0:T(256)} %param.22) | copy-start | bytes 3076
  0.0 25.2 %copy-start.10 = (f32[40]{0:T(128)S(1)}, f32[40]{0:T(128)}, u32[]{:S(2)}) copy-start(f32[40]{0:T(128)} %param.21) | copy-start | bytes 484
  0.0 25.2 %copy-start.8 = (f32[136]{0:T(256)S(1)}, f32[136]{0:T(256)}, u32[]{:S(2)}) copy-start(f32[136]{0:T(256)} %param.20) | copy-start | bytes 1636
  0.1 25.2 %copy-start = (bf16[256,256]{1,0:T(8,128)(2,1)S(1)}, bf16[256,256]{1,0:T(8,128)(2,1)}, u32[]{:S(2)}) copy-start(bf16[256,256]{1,0:T(8,128)(2,1)} %refs_2_.1) | copy-start | bytes 393220
  0.1 25.2 %copy-start.3 = (bf16[40,40]{1,0:T(8,128)(2,1)S(1)}, bf16[40,40]{1,0:T(8,128)(2,1)}, u32[]{:S(2)}) copy-start(bf16[40,40]{1,0:T(8,128)(2,1)} %refs_1_.1) | copy-start | bytes 9604
  0.1 25.2 %copy-start.1 = (bf16[136,136]{1,0:T(8,128)(2,1)S(1)}, bf16[136,136]{1,0:T(8,128)(2,1)}, u32[]{:S(2)}) copy-start(bf16[136,136]{1,0:T(8,128)(2,1)} %refs_0_.2) | copy-start | bytes 110980
  3.6 3.7 %collective-permute-start = (bf16[128,256]{1,0:T(8,128)(2,1)S(1)}, bf16[128,256]{1,0:T(8,128)(2,1)S(1)}, u32[]{:S(2)}, u32[]{:S(2)}) collective-permute-start(bf16[128,256]{1,0:T(8,128)(2,1)S(1)} %get-tuple-element.32), channel_id=1, source_target_pairs={{0,32},{32,64},{64,96},{96,128},{128,160},{160,192},{192,224},{224... | collective-permute-start | bytes 196616 | tf_op jit(solution)/shard_map/ppermute | solution.py:577
  3.6 3.7 %collective-permute-start.1 = (bf16[128,256]{1,0:T(8,128)(2,1)S(1)}, bf16[128,256]{1,0:T(8,128)(2,1)S(1)}, u32[]{:S(2)}, u32[]{:S(2)}) collective-permute-start(bf16[128,256]{1,0:T(8,128)(2,1)S(1)} %get-tuple-element.33), channel_id=1, source_target_pairs={{0,224},{32,0},{64,32},{96,64},{128,96},{160,128},{192,160},{224,1... | collective-permute-start | bytes 196616 | tf_op jit(solution)/shard_map/ppermute | solution.py:577
  7.4 18.5 %collective-permute-start.3 = (bf16[544,256]{1,0:T(8,128)(2,1)S(1)}, bf16[544,256]{1,0:T(8,128)(2,1)S(1)}, u32[]{:S(2)}, u32[]{:S(2)}) collective-permute-start(bf16[544,256]{1,0:T(8,128)(2,1)S(1)} %get-tuple-element.39), channel_id=1, source_target_pairs={{0,31},{1,0},{2,1},{3,2},{4,3},{5,4},{6,5},{7,6},{8,7},{9,8},{10,9... | collective-permute-start | bytes 835592 | tf_op jit(solution)/shard_map/ppermute | solution.py:577
  15.8 12.8 %collective-permute-start.2 = (bf16[544,256]{1,0:T(8,128)(2,1)S(1)}, bf16[544,256]{1,0:T(8,128)(2,1)S(1)}, u32[]{:S(2)}, u32[]{:S(2)}) collective-permute-start(bf16[544,256]{1,0:T(8,128)(2,1)S(1)} %get-tuple-element.38.after), channel_id=1, source_target_pairs={{0,1},{1,2},{2,3},{3,4},{4,5},{5,6},{6,7},{7,8},{8,9},{9,10},{10,1... | collective-permute-start | bytes 835592 | tf_op jit(solution)/shard_map/ppermute | solution.py:577
  15.8 8.6 %all-to-all-start = ((f32[8,4,16]{2,1,0:T(4,128)}), f32[8,4,16]{2,1,0:T(4,128)S(1)}, u32[]{:S(2)}, u32[]{:S(2)}) async-start(f32[8,4,16]{2,1,0:T(4,128)} %shard_map.155.after), calls=%async_computation | async-start | bytes 32768 | tf_op jit(solution)/shard_map/all_to_all | solution.py:581
  37.2 0.6 copy-start.12
  37.8 0.6 copy-start.11
  37.8 29.9 %collective-permute-start.6 = (bf16[512,256]{1,0:T(8,128)(2,1)}, bf16[512,256]{1,0:T(8,128)(2,1)S(1)}, u32[]{:S(2)}, u32[]{:S(2)}) collective-permute-start(bf16[512,256]{1,0:T(8,128)(2,1)} %get-tuple-element.57), channel_id=1, source_target_pairs={{0,1},{1,2},{2,3},{3,4},{4,5},{5,6},{6,7},{7,8},{8,9},{9,10},{10,1... | collective-permute-start | bytes 786440 | tf_op jit(solution)/shard_map/ppermute | solution.py:577
  38.4 29.3 %collective-permute-start.7 = (bf16[512,256]{1,0:T(8,128)(2,1)}, bf16[512,256]{1,0:T(8,128)(2,1)S(1)}, u32[]{:S(2)}, u32[]{:S(2)}) collective-permute-start(bf16[512,256]{1,0:T(8,128)(2,1)} %get-tuple-element.50.refs_6_), channel_id=1, source_target_pairs={{0,31},{1,0},{2,1},{3,2},{4,3},{5,4},{6,5},{7,6},{8,7},{9,8},{10,9... | collective-permute-start | bytes 786440 | tf_op jit(solution)/shard_map/ppermute | solution.py:577
  43.1 13.9 %all-to-all-start.1 = ((f32[32,4,128]{2,1,0:T(4,128)}), f32[32,4,128]{2,1,0:T(4,128)S(1)}, u32[]{:S(2)}, u32[]{:S(2)}) async-start(f32[32,4,128]{2,1,0:T(4,128)} %shard_map.158.refs_7_.after), calls=%async_computation.1 | async-start | bytes 131072 | tf_op jit(solution)/shard_map/all_to_all | solution.py:581
  47.0 12.4 %collective-permute-start.4 = (bf16[160,256]{1,0:T(8,128)(2,1)}, bf16[160,256]{1,0:T(8,128)(2,1)S(1)}, u32[]{:S(2)}, u32[]{:S(2)}) collective-permute-start(bf16[160,256]{1,0:T(8,128)(2,1)} %copy-done.12), channel_id=1, source_target_pairs={{0,32},{32,64},{64,96},{96,128},{128,160},{160,192},{192,224},{224... | collective-permute-start | bytes 245768 | tf_op jit(solution)/shard_map/ppermute | solution.py:577
  47.0 12.4 %collective-permute-start.5 = (bf16[160,256]{1,0:T(8,128)(2,1)}, bf16[160,256]{1,0:T(8,128)(2,1)S(1)}, u32[]{:S(2)}, u32[]{:S(2)}) collective-permute-start(bf16[160,256]{1,0:T(8,128)(2,1)} %copy-done.11), channel_id=1, source_target_pairs={{0,224},{32,0},{64,32},{96,64},{128,96},{160,128},{192,160},{224,1... | collective-permute-start | bytes 245768 | tf_op jit(solution)/shard_map/ppermute | solution.py:577
  59.4 4.2 %collective-permute-start.9 = (bf16[32,256]{1,0:T(8,128)(2,1)S(1)}, bf16[32,256]{1,0:T(8,128)(2,1)S(1)}, u32[]{:S(2)}, u32[]{:S(2)}) collective-permute-start(bf16[32,256]{1,0:T(8,128)(2,1)S(1)} %get-tuple-element.58), channel_id=1, source_target_pairs={{0,31},{1,0},{2,1},{3,2},{4,3},{5,4},{6,5},{7,6},{8,7},{9,8},{10,9... | collective-permute-start | bytes 49160 | tf_op jit(solution)/shard_map/ppermute | solution.py:577
  60.6 7.1 %collective-permute-start.8 = (bf16[32,256]{1,0:T(8,128)(2,1)S(1)}, bf16[32,256]{1,0:T(8,128)(2,1)S(1)}, u32[]{:S(2)}, u32[]{:S(2)}) collective-permute-start(bf16[32,256]{1,0:T(8,128)(2,1)S(1)} %get-tuple-element.53.after), channel_id=1, source_target_pairs={{0,1},{1,2},{2,3},{3,4},{4,5},{5,6},{6,7},{7,8},{8,9},{9,10},{10,1... | collective-permute-start | bytes 49160 | tf_op jit(solution)/shard_map/ppermute | solution.py:577

commit v4 on v3

--- a/solution.py
+++ b/solution.py
@@ -119,23 +119,35 @@
     small.start()
     for c in range(CHUNKS):
         copy(c).start()
+    early = 2
+    per = rows // OWN
+    rims = selection(jnp.zeros((MODES, CY), bf16))[: 2 * RIM]
+
+    def block(k):
+        return buf[k * OWN : (k + 1) * OWN, :].astype(bf16)
+
+    def put_rims(k, out):
+        at = slice(k * RIM, (k + 1) * RIM)
+        rim_lo[at, :] = out[:RIM].astype(bf16)
+        rim_hi[at, :] = out[RIM : 2 * RIM].astype(bf16)
+
+    for c in range(early):
+        copy(c).wait()
+        for k in range(c * per, (c + 1) * per):
+            put_rims(k, dot(rims, block(k)))
     small.wait()
     take = selection(cyt_buf[...])
     sel[...] = take
-    for c in range(CHUNKS):
+    for c in range(early, CHUNKS):
         copy(c).wait()
-        for b in range(rows // OWN):
-            k = c * (rows // OWN) + b
-            data = buf[k * OWN : (k + 1) * OWN, :].astype(bf16)
-            if k == 0:
-                first_x[...] = data
-            if k == BLOCKS - 1:
-                last_x[...] = data
-            out = dot(take, data)
-            at = slice(k * RIM, (k + 1) * RIM)
-            rim_lo[at, :] = out[:RIM].astype(bf16)
-            rim_hi[at, :] = out[RIM : 2 * RIM].astype(bf16)
-            along_y[at, :] = out[2 * RIM :]
+        for k in range(c * per, (c + 1) * per):
+            out = dot(take, block(k))
+            put_rims(k, out)
+            along_y[k * RIM : (k + 1) * RIM, :] = out[2 * RIM :]
+    for k in range(early * per):
+        along_y[k * RIM : (k + 1) * RIM, :] = dot(take[2 * RIM :], block(k))
+    first_x[...] = block(0)
+    last_x[...] = block(BLOCKS - 1)
 
 
 def load(residual, coarse_y):

time: 69.6 us -> 69.3 us (level)
  no operation moved by 1% of the time
where the time goes in v4:
time: 69.3 us; the launch traced here: 69.1 us
  starting transfers between devices  28.2 us (41%)
  Pallas kernels  21.2 us (31%)
  waiting for transfers between devices  18.2 us (26%)
  local copies, waits for them, and re-layouts  1.3 us (2%)
    ppermute x10, starting transfers between devices, shift(): return lax.ppermute(x, axis, [(i, (i + step) % size) for i in range(size)])  18.7 us
    all_to_all x2, waiting for transfers between devices, exchange(): return lax.all_to_all(x, axis, 0, 0)  10.8 us
    all_to_all x2, starting transfers between devices, exchange(): return lax.all_to_all(x, axis, 0, 0)  9.5 us
    pallas_call x1, Pallas kernels, solve(): call(solve_kernel, (sds((BLOCKS * ROWS, NZ), bf16), strip, strip, rim, ri...  8.59 us
    ppermute x10, waiting for transfers between devices, shift(): return lax.ppermute(x, axis, [(i, (i + step) % size) for i in range(size)])  7.39 us
    pallas_call x1, Pallas kernels, load(): call(load_kernel, (sds((OWN, NZ), bf16), sds((OWN, NZ), bf16), rim, rim,...  3.22 us
    pallas_call x1, Pallas kernels, local(): call(coarse_kernel, sds((2 * CX * MODES, NZ), bf16), [VM] * 2 + [HBM] * l...  2.36 us
    pallas_call x1, Pallas kernels, finish(): call(finish_kernel, (sds((CX, CY, NZ), f32), sds((CX, 16, NZ), f32)), [VM...  2.09 us
  transfers between devices with their start and end apart: 12, of which 5 were waited for; matrix products, arithmetic and copies ran while one was open for 0% of the time, Pallas kernels for 11%

profile of v4, /device:TPU:4, one launch (start us, length us, event | category | flops | bytes accessed | tf_op | source)
XLA Modules:
  0.0 69.1 jit_solution(4549749072941291804)
XLA Ops:
  0.0 0.0 copy-start.7
  0.0 0.0 copy-start.2
  0.0 0.0 copy-start.9
  0.0 0.0 copy-start.10
  0.0 0.0 copy-start.8
  0.1 0.0 copy-start
  0.1 0.0 copy-start.3
  0.1 0.0 copy-start.1
  0.1 3.2 %shard_map.154 = (bf16[128,256]{1,0:T(8,128)(2,1)S(1)}, bf16[128,256]{1,0:T(8,128)(2,1)S(1)}, bf16[512,256]{1,0:T(8,128)(2,1)S(1)}, bf16[512,256]{1,0:T(8,128)(2...) custom-call(f32[4096,256]{1,0:T(8,128)} %bitcast.19, bf16[4,32]{1,0:T(4,128)(2,1)} %bitcast.12), custom_call_target="tpu_custom_call" | custom-call | tf_op jit(solution)/shard_map/pallas_call | solution.py:155
  3.3 0.0 collective-permute-start
  3.3 1.7 %collective-permute-start.1 = (bf16[128,256]{1,0:T(8,128)(2,1)S(1)}, bf16[128,256]{1,0:T(8,128)(2,1)S(1)}, u32[]{:S(2)}, u32[]{:S(2)}) collective-permute-start(bf16[128,256]{1,0:T(8,128)(2,1)S(1)} %get-tuple-element.33), channel_id=1, source_target_pairs={{0,224},{32,0},{64,32},{96,64},{128,96},{160,128},{192,160},{224,1... | collective-permute-start | bytes 196616 | tf_op jit(solution)/shard_map/ppermute | solution.py:589
  5.1 0.0 copy-done.6
  5.1 1.3 %shard_map.155.after = f32[8,4,16]{2,1,0:T(4,128)} custom-call(f32[512,256]{1,0:T(8,128)S(1)} %get-tuple-element.37.along_y, bf16[4,128]{1,0:T(4,128)(2,1)S(1)} %bitcast.15, bf16[4,256]{1,0:T(4,128)(2,1)S(1)} %bitcast.11), custom_call_target="tpu_custom_call" | custom-call | tf_op jit(solution)/shard_map/pallas_call | solution.py:604
  6.4 0.6 collective-permute-done.xlo
  7.0 0.0 collective-permute-done.1.xhi
  7.0 0.1 shard_map.156
  7.2 8.3 %collective-permute-start.3 = (bf16[544,256]{1,0:T(8,128)(2,1)S(1)}, bf16[544,256]{1,0:T(8,128)(2,1)S(1)}, u32[]{:S(2)}, u32[]{:S(2)}) collective-permute-start(bf16[544,256]{1,0:T(8,128)(2,1)S(1)} %get-tuple-element.39), channel_id=1, source_target_pairs={{0,31},{1,0},{2,1},{3,2},{4,3},{5,4},{6,5},{7,6},{8,7},{9,8},{10,9... | collective-permute-start | bytes 835592 | tf_op jit(solution)/shard_map/ppermute | solution.py:589
  15.5 0.0 collective-permute-start.2
  15.5 5.7 %all-to-all-start = ((f32[8,4,16]{2,1,0:T(4,128)}), f32[8,4,16]{2,1,0:T(4,128)S(1)}, u32[]{:S(2)}, u32[]{:S(2)}) async-start(f32[8,4,16]{2,1,0:T(4,128)} %shard_map.155.after), calls=%async_computation | async-start | bytes 32768 | tf_op jit(solution)/shard_map/all_to_all | solution.py:593
  21.2 0.0 copy-done.7
  21.2 0.4 shard_map.157.modes_xz
  21.6 2.5 %all-to-all-done.rows = f32[8,4,16]{2,1,0:T(4,128)S(1)} async-done(((f32[8,4,16]{2,1,0:T(4,128)}), f32[8,4,16]{2,1,0:T(4,128)S(1)}, u32[]{:S(2)}, u32[]{:S(2)}) %all-to-all-start) | async-done | bytes 2080 | tf_op jit(solution)/shard_map/all_to_all | solution.py:593
  24.1 0.9 %shard_map.158.refs_7_.after = f32[32,4,128]{2,1,0:T(4,128)} custom-call(f32[8,4,16]{2,1,0:T(4,128)S(1)} %all-to-all-done.rows, f32[128,128]{1,0:T(8,128)S(1)} %shard_map.157.modes_xz), custom_call_target="tpu_custom_call" | custom-call | tf_op jit(solution)/shard_map/pallas_call | solution.py:612
  25.0 0.0 copy-done.10
  25.0 0.6 shard_map.159
  25.6 0.0 collective-permute-done.3.yhi
  25.6 2.7 %collective-permute-done.2.ylo = bf16[544,256]{1,0:T(8,128)(2,1)S(1)} collective-permute-done((bf16[544,256]{1,0:T(8,128)(2,1)S(1)}, bf16[544,256]{1,0:T(8,128)(2,1)S(1)}, u32[]{:S(2)}, u32[]{:S(2)}) %collective-permute-start.2) | collective-permute-done | bytes 278560 | tf_op jit(solution)/shard_map/ppermute | solution.py:589
  28.3 8.6 %shard_map.160 = (bf16[5120,256]{1,0:T(8,128)(2,1)S(1)}, bf16[160,256]{1,0:T(8,128)(2,1)S(1)}, bf16[160,256]{1,0:T(8,128)(2,1)S(1)}, bf16[512,256]{1,0:T(8,128)(2,1)}, bf16[512,256]{1,0:T(8,128)(2,1)}) custom-call(f32[4096,256]{1,0:T(8,128)} %bitcast.20, bf16[128,256]{1,0:T(8,128)(2,1)S(1)} %collective-permute-done.xlo, ...), custom_call_target="tpu_custom_call" | custom-call | tf_op jit(solution)/shard_map/pallas_call | solution.py:395
  36.9 0.0 copy-start.12
  36.9 0.6 copy-done.12
  37.5 0.0 collective-permute-start.6
  37.5 0.6 copy-done.11
  38.2 4.7 %collective-permute-start.7 = (bf16[512,256]{1,0:T(8,128)(2,1)}, bf16[512,256]{1,0:T(8,128)(2,1)S(1)}, u32[]{:S(2)}, u32[]{:S(2)}) collective-permute-start(bf16[512,256]{1,0:T(8,128)(2,1)} %get-tuple-element.50.refs_6_), channel_id=1, source_target_pairs={{0,31},{1,0},{2,1},{3,2},{4,3},{5,4},{6,5},{7,6},{8,7},{9,8},{10,9... | collective-permute-start | bytes 786440 | tf_op jit(solution)/shard_map/ppermute | solution.py:589
  42.9 3.8 %all-to-all-start.1 = ((f32[32,4,128]{2,1,0:T(4,128)}), f32[32,4,128]{2,1,0:T(4,128)S(1)}, u32[]{:S(2)}, u32[]{:S(2)}) async-start(f32[32,4,128]{2,1,0:T(4,128)} %shard_map.158.refs_7_.after), calls=%async_computation.1 | async-start | bytes 131072 | tf_op jit(solution)/shard_map/all_to_all | solution.py:593
  46.7 0.0 collective-permute-start.4
  46.8 1.7 %collective-permute-start.5 = (bf16[160,256]{1,0:T(8,128)(2,1)}, bf16[160,256]{1,0:T(8,128)(2,1)S(1)}, u32[]{:S(2)}, u32[]{:S(2)}) collective-permute-start(bf16[160,256]{1,0:T(8,128)(2,1)} %copy-done.11), channel_id=1, source_target_pairs={{0,224},{32,0},{64,32},{96,64},{128,96},{160,128},{192,160},{224,1... | collective-permute-start | bytes 245768 | tf_op jit(solution)/shard_map/ppermute | solution.py:589
  48.5 8.3 %all-to-all-done.1.rows = f32[32,4,128]{2,1,0:T(4,128)S(1)} async-done(((f32[32,4,128]{2,1,0:T(4,128)}), f32[32,4,128]{2,1,0:T(4,128)S(1)}, u32[]{:S(2)}, u32[]{:S(2)}) %all-to-all-start.1) | async-done | bytes 65568 | tf_op jit(solution)/shard_map/all_to_all | solution.py:593
  56.8 2.4 %shard_map.161.after.shape = bf16[1024,256]{1,0:T(8,128)(2,1)S(1)} custom-call(f32[32,4,128]{2,1,0:T(4,128)S(1)} %all-to-all-done.1.rows, f32[128,128]{1,0:T(8,128)S(1)} %shard_map.157.modes_xz, f32[128,128]{1,0:T(8,128)} %refs_0_.3, f32[1,32]{1,0:T(1,128)} %bitcast.21, f32[1,128]{1,0:T(1,128)} %bitcast.22, f32[1,4]{1,0:T(1,128)} %bitcast.23, ...), custom_call_target="tpu_custom_call" | custom-call | tf_op jit(solution)/shard_map/pallas_call | solution.py:633
  59.1 0.0 collective-permute-done.4.rxlo
  59.1 0.0 collective-permute-done.5.rxhi
  59.2 1.2 %collective-permute-start.9 = (bf16[32,256]{1,0:T(8,128)(2,1)S(1)}, bf16[32,256]{1,0:T(8,128)(2,1)S(1)}, u32[]{:S(2)}, u32[]{:S(2)}) collective-permute-start(bf16[32,256]{1,0:T(8,128)(2,1)S(1)} %get-tuple-element.58), channel_id=1, source_target_pairs={{0,31},{1,0},{2,1},{3,2},{4,3},{5,4},{6,5},{7,6},{8,7},{9,8},{10,9... | collective-permute-start | bytes 49160 | tf_op jit(solution)/shard_map/ppermute | solution.py:589
  60.4 0.9 %collective-permute-start.8 = (bf16[32,256]{1,0:T(8,128)(2,1)S(1)}, bf16[32,256]{1,0:T(8,128)(2,1)S(1)}, u32[]{:S(2)}, u32[]{:S(2)}) collective-permute-start(bf16[32,256]{1,0:T(8,128)(2,1)S(1)} %get-tuple-element.53.after), channel_id=1, source_target_pairs={{0,1},{1,2},{2,3},{3,4},{4,5},{5,6},{6,7},{7,8},{8,9},{9,10},{10,1... | collective-permute-start | bytes 49160 | tf_op jit(solution)/shard_map/ppermute | solution.py:589
  61.3 2.1 %shard_map.163 = (f32[128,32,256]{2,1,0:T(8,128)}, f32[128,16,256]{2,1,0:T(8,128)S(1)}) custom-call(bf16[5120,256]{1,0:T(8,128)(2,1)S(1)} %get-tuple-element.48.field, bf16[128,192]{1,0:T(8,128)(2,1)S(1)} %get-tuple-element.49.wfin, bf16[1024,256]{1,0:T(8,128)(2,1)S(1)} %shard_map.161.after.shape, bf16[160,256]{1,0:T(8,128)(2,1)S(1)} %collective-permute-done.4.rxlo, ...), custom_call_target="tpu_custom_call" | custom-call | tf_op jit(solution)/shard_map/pallas_call | solution.py:530
  63.4 0.0 collective-permute-done.9.cornhi
  63.4 4.1 %collective-permute-done.8.cornlo = bf16[32,256]{1,0:T(8,128)(2,1)S(1)} collective-permute-done((bf16[32,256]{1,0:T(8,128)(2,1)S(1)}, bf16[32,256]{1,0:T(8,128)(2,1)S(1)}, u32[]{:S(2)}, u32[]{:S(2)}) %collective-permute-start.8) | collective-permute-done | bytes 16416 | tf_op jit(solution)/shard_map/ppermute | solution.py:589
  67.4 0.0 collective-permute-done.6.rylo
  67.4 0.0 collective-permute-done.7.ryhi
  67.4 1.6 %combine.1 = f32[128,32,256]{2,1,0:T(8,128)} custom-call(f32[128,32,256]{2,1,0:T(8,128)} %get-tuple-element.54.partial, f32[128,16,256]{2,1,0:T(8,128)S(1)} %get-tuple-element.55.rims, bf16[64,32]{1,0:T(8,128)(2,1)S(1)} %get-tuple-element.56.spread, bf16[512,256]{1,0:T(8,128)(2,1)S(1)} %collective-permute-done.6.rylo, ...), custom_call_target="tpu_custom_call", output_to_operand_aliasing={{}: (0, {})} | custom-call | tf_op jit(solution)/shard_map/combine/pallas_call | solution.py:575
  (13 shorter events, 0.0 us)
Async XLA Ops:
  0.0 25.0 %copy-start.5 = (bf16[32,4]{0,1:T(4,128)(2,1)S(1)}, bf16[32,4]{0,1:T(4,128)(2,1)}, u32[]{:S(2)}) copy-start(bf16[32,4]{0,1:T(4,128)(2,1)} %param.24) | copy-start | bytes 772
  0.0 5.1 %copy-start.4 = (bf16[256,4]{0,1:T(4,128)(2,1)S(1)}, bf16[256,4]{0,1:T(4,128)(2,1)}, u32[]{:S(2)}) copy-start(bf16[256,4]{0,1:T(4,128)(2,1)} %param.25) | copy-start | bytes 6148
  0.0 5.1 %copy-start.6 = (bf16[128,4]{0,1:T(4,128)(2,1)S(1)}, bf16[128,4]{0,1:T(4,128)(2,1)}, u32[]{:S(2)}) copy-start(bf16[128,4]{0,1:T(4,128)(2,1)} %param.23) | copy-start | bytes 3076
  0.0 21.2 %copy-start.7 = (f32[4,4]{1,0:T(4,128)S(1)}, f32[4,4]{1,0:T(4,128)}, u32[]{:S(2)}) copy-start(f32[4,4]{1,0:T(4,128)} %mode_z.1) | copy-start | bytes 196
  0.0 21.2 %copy-start.2 = (f32[32,32]{1,0:T(8,128)S(1)}, f32[32,32]{1,0:T(8,128)}, u32[]{:S(2)}) copy-start(f32[32,32]{1,0:T(8,128)} %mode_x.1) | copy-start | bytes 12292
  0.0 25.0 %copy-start.9 = (f32[256]{0:T(256)S(1)}, f32[256]{0:T(256)}, u32[]{:S(2)}) copy-start(f32[256]{0:T(256)} %param.22) | copy-start | bytes 3076
  0.0 25.0 %copy-start.10 = (f32[40]{0:T(128)S(1)}, f32[40]{0:T(128)}, u32[]{:S(2)}) copy-start(f32[40]{0:T(128)} %param.21) | copy-start | bytes 484
  0.0 25.0 %copy-start.8 = (f32[136]{0:T(256)S(1)}, f32[136]{0:T(256)}, u32[]{:S(2)}) copy-start(f32[136]{0:T(256)} %param.20) | copy-start | bytes 1636
  0.1 24.9 %copy-start = (bf16[256,256]{1,0:T(8,128)(2,1)S(1)}, bf16[256,256]{1,0:T(8,128)(2,1)}, u32[]{:S(2)}) copy-start(bf16[256,256]{1,0:T(8,128)(2,1)} %refs_2_.1) | copy-start | bytes 393220
  0.1 24.9 %copy-start.3 = (bf16[40,40]{1,0:T(8,128)(2,1)S(1)}, bf16[40,40]{1,0:T(8,128)(2,1)}, u32[]{:S(2)}) copy-start(bf16[40,40]{1,0:T(8,128)(2,1)} %refs_1_.1) | copy-start | bytes 9604
  0.1 24.9 %copy-start.1 = (bf16[136,136]{1,0:T(8,128)(2,1)S(1)}, bf16[136,136]{1,0:T(8,128)(2,1)}, u32[]{:S(2)}) copy-start(bf16[136,136]{1,0:T(8,128)(2,1)} %refs_0_.2) | copy-start | bytes 110980
  3.3 3.7 %collective-permute-start = (bf16[128,256]{1,0:T(8,128)(2,1)S(1)}, bf16[128,256]{1,0:T(8,128)(2,1)S(1)}, u32[]{:S(2)}, u32[]{:S(2)}) collective-permute-start(bf16[128,256]{1,0:T(8,128)(2,1)S(1)} %get-tuple-element.32), channel_id=1, source_target_pairs={{0,32},{32,64},{64,96},{96,128},{128,160},{160,192},{192,224},{224... | collective-permute-start | bytes 196616 | tf_op jit(solution)/shard_map/ppermute | solution.py:589
  3.3 3.7 %collective-permute-start.1 = (bf16[128,256]{1,0:T(8,128)(2,1)S(1)}, bf16[128,256]{1,0:T(8,128)(2,1)S(1)}, u32[]{:S(2)}, u32[]{:S(2)}) collective-permute-start(bf16[128,256]{1,0:T(8,128)(2,1)S(1)} %get-tuple-element.33), channel_id=1, source_target_pairs={{0,224},{32,0},{64,32},{96,64},{128,96},{160,128},{192,160},{224,1... | collective-permute-start | bytes 196616 | tf_op jit(solution)/shard_map/ppermute | solution.py:589
  7.2 18.5 %collective-permute-start.3 = (bf16[544,256]{1,0:T(8,128)(2,1)S(1)}, bf16[544,256]{1,0:T(8,128)(2,1)S(1)}, u32[]{:S(2)}, u32[]{:S(2)}) collective-permute-start(bf16[544,256]{1,0:T(8,128)(2,1)S(1)} %get-tuple-element.39), channel_id=1, source_target_pairs={{0,31},{1,0},{2,1},{3,2},{4,3},{5,4},{6,5},{7,6},{8,7},{9,8},{10,9... | collective-permute-start | bytes 835592 | tf_op jit(solution)/shard_map/ppermute | solution.py:589
  15.5 12.8 %collective-permute-start.2 = (bf16[544,256]{1,0:T(8,128)(2,1)S(1)}, bf16[544,256]{1,0:T(8,128)(2,1)S(1)}, u32[]{:S(2)}, u32[]{:S(2)}) collective-permute-start(bf16[544,256]{1,0:T(8,128)(2,1)S(1)} %get-tuple-element.38.after), channel_id=1, source_target_pairs={{0,1},{1,2},{2,3},{3,4},{4,5},{5,6},{6,7},{7,8},{8,9},{9,10},{10,1... | collective-permute-start | bytes 835592 | tf_op jit(solution)/shard_map/ppermute | solution.py:589
  15.5 8.6 %all-to-all-start = ((f32[8,4,16]{2,1,0:T(4,128)}), f32[8,4,16]{2,1,0:T(4,128)S(1)}, u32[]{:S(2)}, u32[]{:S(2)}) async-start(f32[8,4,16]{2,1,0:T(4,128)} %shard_map.155.after), calls=%async_computation | async-start | bytes 32768 | tf_op jit(solution)/shard_map/all_to_all | solution.py:593
  36.9 0.6 copy-start.12
  37.5 0.6 copy-start.11
  37.5 29.9 %collective-permute-start.6 = (bf16[512,256]{1,0:T(8,128)(2,1)}, bf16[512,256]{1,0:T(8,128)(2,1)S(1)}, u32[]{:S(2)}, u32[]{:S(2)}) collective-permute-start(bf16[512,256]{1,0:T(8,128)(2,1)} %get-tuple-element.57), channel_id=1, source_target_pairs={{0,1},{1,2},{2,3},{3,4},{4,5},{5,6},{6,7},{7,8},{8,9},{9,10},{10,1... | collective-permute-start | bytes 786440 | tf_op jit(solution)/shard_map/ppermute | solution.py:589
  38.2 29.3 %collective-permute-start.7 = (bf16[512,256]{1,0:T(8,128)(2,1)}, bf16[512,256]{1,0:T(8,128)(2,1)S(1)}, u32[]{:S(2)}, u32[]{:S(2)}) collective-permute-start(bf16[512,256]{1,0:T(8,128)(2,1)} %get-tuple-element.50.refs_6_), channel_id=1, source_target_pairs={{0,31},{1,0},{2,1},{3,2},{4,3},{5,4},{6,5},{7,6},{8,7},{9,8},{10,9... | collective-permute-start | bytes 786440 | tf_op jit(solution)/shard_map/ppermute | solution.py:589
  42.9 13.9 %all-to-all-start.1 = ((f32[32,4,128]{2,1,0:T(4,128)}), f32[32,4,128]{2,1,0:T(4,128)S(1)}, u32[]{:S(2)}, u32[]{:S(2)}) async-start(f32[32,4,128]{2,1,0:T(4,128)} %shard_map.158.refs_7_.after), calls=%async_computation.1 | async-start | bytes 131072 | tf_op jit(solution)/shard_map/all_to_all | solution.py:593
  46.7 12.4 %collective-permute-start.4 = (bf16[160,256]{1,0:T(8,128)(2,1)}, bf16[160,256]{1,0:T(8,128)(2,1)S(1)}, u32[]{:S(2)}, u32[]{:S(2)}) collective-permute-start(bf16[160,256]{1,0:T(8,128)(2,1)} %copy-done.12), channel_id=1, source_target_pairs={{0,32},{32,64},{64,96},{96,128},{128,160},{160,192},{192,224},{224... | collective-permute-start | bytes 245768 | tf_op jit(solution)/shard_map/ppermute | solution.py:589
  46.8 12.4 %collective-permute-start.5 = (bf16[160,256]{1,0:T(8,128)(2,1)}, bf16[160,256]{1,0:T(8,128)(2,1)S(1)}, u32[]{:S(2)}, u32[]{:S(2)}) collective-permute-start(bf16[160,256]{1,0:T(8,128)(2,1)} %copy-done.11), channel_id=1, source_target_pairs={{0,224},{32,0},{64,32},{96,64},{128,96},{160,128},{192,160},{224,1... | collective-permute-start | bytes 245768 | tf_op jit(solution)/shard_map/ppermute | solution.py:589
  59.2 4.2 %collective-permute-start.9 = (bf16[32,256]{1,0:T(8,128)(2,1)S(1)}, bf16[32,256]{1,0:T(8,128)(2,1)S(1)}, u32[]{:S(2)}, u32[]{:S(2)}) collective-permute-start(bf16[32,256]{1,0:T(8,128)(2,1)S(1)} %get-tuple-element.58), channel_id=1, source_target_pairs={{0,31},{1,0},{2,1},{3,2},{4,3},{5,4},{6,5},{7,6},{8,7},{9,8},{10,9... | collective-permute-start | bytes 49160 | tf_op jit(solution)/shard_map/ppermute | solution.py:589
  60.4 7.1 %collective-permute-start.8 = (bf16[32,256]{1,0:T(8,128)(2,1)S(1)}, bf16[32,256]{1,0:T(8,128)(2,1)S(1)}, u32[]{:S(2)}, u32[]{:S(2)}) collective-permute-start(bf16[32,256]{1,0:T(8,128)(2,1)S(1)} %get-tuple-element.53.after), channel_id=1, source_target_pairs={{0,1},{1,2},{2,3},{3,4},{4,5},{5,6},{6,7},{7,8},{8,9},{9,10},{10,1... | collective-permute-start | bytes 49160 | tf_op jit(solution)/shard_map/ppermute | solution.py:589
